TPU v7x, 32 devices: a whole 2x2x4 slice. The times are simulated.
32 devices in a mesh: groups: 2 (over x), seq: 8 (over z, y), pipe: 2 (over core).
Axes of the slice: x: 2, y: 2, z: 4, core: 2. Of those that a mesh axis runs over, the one named last changes fastest.
Arguments:
- tokens: bfloat16 [2, 2048, 1440], P('pipe', ('groups', 'seq')), parts along dimension 1, may hold values from -6 to 6
- routes: int32 [2, 2048, 4], P('pipe', ('groups', 'seq')), parts along dimension 1, may hold values from 0 to 15, all different within a row; in each aligned block of 128 rows (0 to 127, 128 to 255, ..., all dimensions but the last counted through in order) at most 48 rows name the same one
- route_weights: float32 [2, 2048, 4], P('pipe', ('groups', 'seq')), parts along dimension 1, may hold values from 0.1 to 1
- moe_gain: float32 [1440], replicated, may hold values from 0.5 to 1.5
- gate_up: bfloat16 [32, 1440, 1440], P('seq'), may hold values from -0.15625 to 0.15625
- down_proj: bfloat16 [32, 720, 1440], P('seq'), may hold values from -0.15625 to 0.15625
- attn_gain: float32 [1440], replicated, may hold values from 0.5 to 1.5
- qkv_proj: bfloat16 [1440, 2560], P('seq'), may hold values from -0.15625 to 0.15625
- head_sink_logits: float32 [32], replicated, may hold values from 3 to 6
- out_proj: bfloat16 [2048, 1440], P('seq'), may hold values from -0.125 to 0.125
Outputs:
- layer_output: bfloat16 [2, 2048, 1440], P('pipe', ('groups', 'seq')), parts along dimension 1
There are 2 independent parts, one for each index of `groups`. A program takes and returns all parts, laid end to end along the dimension named above; an argument that names none is the same for every part. Nothing has to cross between parts.
Inputs may be any that keep to these rules, and one draw needn't show every extreme that they name: `routes`: within the 128 positions of one micro-batch on one index of seq, a token names each of its 4 experts once, and each expert is named by at most 48 tokens; one expert is named by exactly 48 of them.
All inputs are finite; a program needn't handle non-finite values.
Results may differ from a plain program's by a relative error of at most 0.0085.
Values may be sent and summed in bfloat16 or wider, within the bound.
A program may use at most 128 MiB of HBM per device.

v0:
```python
import functools

import jax
import jax.numpy as jnp
from jax import lax
from jax.experimental import pallas as pl
from jax.experimental.pallas import tpu as pltpu
from jax.sharding import PartitionSpec as P

MESH = pl.DeviceIdType.MESH
E = 16
TOP = 4
QUERY_HEADS = 32
KEY_VALUE_HEADS = 4
HEAD_SIZE = 64
WINDOW_SPAN = 128
HALF = 720
CAP = 48


eps = 1e-05


def from_partner(value, axis, distance):
    return lax.ppermute(value, axis, [(i, i ^ 1 << distance) for i in range(lax.axis_size(axis))])


def shifted(value, axis, steps):
    count = lax.axis_size(axis)
    pairs = [(source, (source + steps) % count) for source in range(count)]
    return lax.ppermute(value, axis, pairs)


def passed_along(value, axis, steps):
    count = lax.axis_size(axis)
    first, last = (max(0, -steps), min(count, count - steps))
    return lax.ppermute(value, axis, [(source, source + steps) for source in range(first, last)])


def rms_scale(value_matrix, gain):
    widened = value_matrix.astype(jnp.float32)
    mean_square = jnp.mean(widened * widened, axis=-1, keepdims=True)
    return (widened * lax.rsqrt(mean_square + eps) * gain).astype(jnp.bfloat16)


def slot_positions(route_rows):
    flat = route_rows.reshape(-1)
    onehot = (flat[:, None] == jnp.arange(E, dtype=jnp.int32)[None, :]).astype(jnp.int32)
    earlier = jnp.cumsum(onehot, axis=0) - onehot
    return flat * CAP + jnp.sum(earlier * onehot, axis=1)


def expert_layer(local, route_rows, route_scale, moe_gain, gate_up, down_proj):
    tok_count, width = local.shape
    seq_count = lax.axis_size("seq")
    per_device = gate_up.shape[0]
    normed = rms_scale(local, moe_gain)
    positions = slot_positions(route_rows)
    select = (positions[None, :] == jnp.arange(E * CAP, dtype=jnp.int32)[:, None]).astype(
        jnp.bfloat16
    )
    repeated = jnp.repeat(normed, TOP, axis=0)
    table = jnp.dot(select, repeated, preferred_element_type=jnp.float32).astype(jnp.bfloat16)
    by_expert = table.reshape(E, CAP, width)
    first = lax.axis_index("seq") % 2 == 0
    outgoing = jnp.repeat(by_expert, 2, axis=0).reshape(seq_count, per_device, CAP, width)
    received = lax.all_to_all(outgoing, "seq", split_axis=0, concat_axis=0, tiled=True)
    projected = jnp.einsum("spcd,pdh->spch", received, gate_up, preferred_element_type=jnp.float32)
    gate_part = projected[..., :HALF]
    up_part = projected[..., HALF:]
    hidden = (gate_part * jax.nn.sigmoid(1.702 * gate_part) * (up_part + 1.0)).astype(jnp.bfloat16)
    partial_value = jnp.einsum(
        "spch,phd->spcd", hidden, down_proj, preferred_element_type=jnp.float32
    )
    if per_device >= 2:
        finished = (
            partial_value.reshape(seq_count, per_device // 2, 2, CAP, width)
            .sum(axis=2)
            .astype(jnp.bfloat16)
        )
    else:
        lower_rows = partial_value[:, :, : CAP // 2]
        upper_rows = partial_value[:, :, CAP // 2 :]
        kept = jnp.where(first, lower_rows, upper_rows)
        given = jnp.where(first, upper_rows, lower_rows)
        partner_part = from_partner(given.astype(jnp.bfloat16), "seq", 0).astype(given.dtype)
        finished = (kept + partner_part).astype(jnp.bfloat16)
    summed = lax.all_to_all(finished, "seq", split_axis=0, concat_axis=0, tiled=True).reshape(
        E * CAP, width
    )
    picked = lax.dot_general(
        select, summed, (((0,), (0,)), ((), ())), preferred_element_type=jnp.float32
    )
    weighted = jnp.sum(picked.reshape(tok_count, TOP, width) * route_scale[:, :, None], axis=1)
    return (local.astype(jnp.float32) + weighted).astype(jnp.bfloat16)


def attend(query_matrix, keys_extended, values_extended, head_sink_logits, halo_valid):
    tok_count = query_matrix.shape[0]
    query_groups = QUERY_HEADS // KEY_VALUE_HEADS
    attention_block = min(tok_count, 512)
    scale = float(HEAD_SIZE) ** (-0.5)
    sink_mass_total = jnp.exp(head_sink_logits).reshape(KEY_VALUE_HEADS, query_groups, 1, 1)
    block_queries = query_matrix.reshape(attention_block, KEY_VALUE_HEADS, query_groups, HEAD_SIZE)
    block_keys = keys_extended.reshape(attention_block + WINDOW_SPAN, KEY_VALUE_HEADS, HEAD_SIZE)
    block_values = values_extended.reshape(
        attention_block + WINDOW_SPAN, KEY_VALUE_HEADS, HEAD_SIZE
    )
    scores = (
        jnp.einsum("qhgd,khd->hgqk", block_queries, block_keys, preferred_element_type=jnp.float32)
        * scale
    )
    query_pos = jnp.arange(attention_block, dtype=jnp.int32)[:, None] + WINDOW_SPAN
    key_pos = jnp.arange(attention_block + WINDOW_SPAN, dtype=jnp.int32)[None, :]
    distance = query_pos - key_pos
    allowed = (
        (distance >= 0) & (distance < WINDOW_SPAN) & ((key_pos + 0 >= WINDOW_SPAN) | halo_valid)
    )
    weights = jnp.where(allowed, jnp.exp(scores), 0.0)
    probs = (weights / (jnp.sum(weights, axis=-1, keepdims=True) + sink_mass_total)).astype(
        jnp.bfloat16
    )
    mixed = jnp.einsum("hgqk,khd->qhgd", probs, block_values, preferred_element_type=jnp.float32)
    outputs = mixed.reshape(attention_block, QUERY_HEADS * HEAD_SIZE).astype(jnp.bfloat16)
    return outputs


def body(
    tokens,
    routes,
    route_weights,
    moe_gain,
    gate_up,
    down_proj,
    attn_gain,
    qkv_proj,
    head_sink_logits,
    out_proj,
):
    hidden = expert_layer(tokens[0], routes[0], route_weights[0], moe_gain, gate_up, down_proj)
    tok_count, width = hidden.shape
    normed = rms_scale(hidden, attn_gain)
    seq_index = lax.axis_index("seq")
    pipe_index = lax.axis_index("pipe")
    halo_valid = (seq_index > 0) | (pipe_index > 0)
    query_width = QUERY_HEADS * HEAD_SIZE
    width_of_pair = KEY_VALUE_HEADS * HEAD_SIZE
    columns = normed
    packed_heads = jnp.dot(
        columns,
        lax.all_gather(qkv_proj, "seq", axis=0, tiled=True),
        preferred_element_type=jnp.float32,
    ).astype(jnp.bfloat16)
    from_left = shifted(packed_heads[tok_count - WINDOW_SPAN :, query_width:], "seq", 1)
    from_section = passed_along(from_left, "pipe", 1)
    halo_pairs = jnp.where(seq_index == 0, from_section, from_left)
    query_matrix = packed_heads[:, :query_width]
    pairs_ext = jnp.concatenate([halo_pairs, packed_heads[:, query_width:]], axis=0)
    keys_extended = pairs_ext[:, :width_of_pair]
    values_extended = pairs_ext[:, width_of_pair:]
    attended = attend(query_matrix, keys_extended, values_extended, head_sink_logits, halo_valid)
    columns = attended
    projected = jnp.dot(
        columns,
        lax.all_gather(out_proj, "seq", axis=0, tiled=True),
        preferred_element_type=jnp.float32,
    )
    return (hidden.astype(jnp.float32) + projected).astype(jnp.bfloat16)[None]


def ring_place(index, count, folded):
    if not folded:
        return index
    line, side = index // 2, index % 2
    return line + side * (count - 1 - 2 * line)

def ring_index(place, count, folded):
    if not folded:
        return place
    side = place // (count // 2)
    line = place + side * (count - 1 - 2 * place)
    return 2 * line + side

def greet(peers):
    barrier = pltpu.get_barrier_semaphore()
    for peer in peers:
        pl.semaphore_signal(barrier, inc=1, device_id={"seq": peer}, device_id_type=MESH)
    pl.semaphore_wait(barrier, len(peers))

def remote(src, dst, send, recv, peer):
    return pltpu.make_async_remote_copy(src_ref=src, dst_ref=dst, send_sem=send, recv_sem=recv,
        device_id={"seq": peer}, device_id_type=MESH)

def gather_kernel(count, folded, own_ref, all_ref, send_sem, recv_sem):
    me = lax.axis_index("seq")
    place = ring_place(me, count, folded)
    at = lambda offset: ring_index(lax.rem(place + offset + count, count), count, folded)
    peers = (at(1), at(-1))
    greet(peers)
    rows = own_ref.shape[0]
    steps = count // 2
    copies = []
    for step in range(steps):
        for way in (0, 1):
            origin = at(-step if way == 0 else step)
            part = pl.ds(way * (rows // 2), rows // 2) if step == steps - 1 else pl.ds(0, rows)
            if step:
                copies[2 * (step - 1) + way].wait_recv()
            src = all_ref.at[origin, part] if step else own_ref.at[part]
            copy = remote(src, all_ref.at[origin, part], send_sem.at[way, step], recv_sem.at[way, step], peers[way])
            copy.start()
            copies.append(copy)
        if step == 0:
            all_ref[me] = own_ref[...]
    for copy in copies[-2:]:
        copy.wait_recv()
    for copy in copies:
        copy.wait_send()

def ring_gather(own, folded, cid):
    count = lax.axis_size("seq")
    steps = count // 2
    return pl.pallas_call(functools.partial(gather_kernel, count, folded),
        out_shape=jax.ShapeDtypeStruct((count,) + own.shape, own.dtype),
        in_specs=[pl.BlockSpec(memory_space=pltpu.VMEM)],
        out_specs=pl.BlockSpec(memory_space=pltpu.VMEM),
        scratch_shapes=[pltpu.SemaphoreType.DMA((2, steps)), pltpu.SemaphoreType.DMA((2, steps))],
        compiler_params=pltpu.CompilerParams(collective_id=cid, has_side_effects=True))(own)

def scatter_kernel(count, folded, part_ref, out_ref, held, send_sem, recv_sem):
    me = lax.axis_index("seq")
    place = ring_place(me, count, folded)
    at = lambda offset: ring_index(lax.rem(place + offset + count, count), count, folded)
    peers = (at(1), at(-1))
    greet(peers)
    rows = part_ref.shape[1]
    half = rows // 2
    steps = count // 2
    copies = []
    for step in range(steps):
        for way in (0, 1):
            goal = at((steps - step) * (1 if way == 0 else -1))
            whole = pl.ds(way * half, half) if step == 0 else pl.ds(0, rows)
            if step == 0:
                src = part_ref.at[goal, whole]
            else:
                copies[2 * (step - 1) + way].wait_recv()
                src = held.at[way, step - 1]
                if step == 1:
                    mine, other = pl.ds(way * half, half), pl.ds((1 - way) * half, half)
                    held[way, 0, mine] = (held[way, 0, mine].astype(jnp.float32) + part_ref[goal, mine].astype(jnp.float32)).astype(held.dtype)
                    held[way, 0, other] = part_ref[goal, other]
                else:
                    held[way, step - 1] = (held[way, step - 1].astype(jnp.float32) + part_ref[goal].astype(jnp.float32)).astype(held.dtype)
            copy = remote(src, held.at[way, step, whole], send_sem.at[way, step], recv_sem.at[way, step], peers[way])
            copy.start()
            copies.append(copy)
    for copy in copies[-2:]:
        copy.wait_recv()
    out_ref[...] = part_ref[me].astype(jnp.float32) + held[0, steps - 1].astype(jnp.float32) + held[1, steps - 1].astype(jnp.float32)
    for copy in copies:
        copy.wait_send()

def ring_scatter(parts, folded, cid):
    count = lax.axis_size("seq")
    steps = count // 2
    rows, width = parts.shape[1:]
    return pl.pallas_call(functools.partial(scatter_kernel, count, folded),
        out_shape=jax.ShapeDtypeStruct((rows, width), jnp.float32),
        in_specs=[pl.BlockSpec(memory_space=pltpu.VMEM)],
        out_specs=pl.BlockSpec(memory_space=pltpu.VMEM),
        scratch_shapes=[pltpu.VMEM((2, steps, rows, width), parts.dtype),
            pltpu.SemaphoreType.DMA((2, steps)), pltpu.SemaphoreType.DMA((2, steps))],
        compiler_params=pltpu.CompilerParams(collective_id=cid, has_side_effects=True, vmem_limit_bytes=40 << 20))(parts)


def exchanged(value):
    return lax.ppermute(value, "pipe", [(0, 1), (1, 0)])


def experts_by_rings(local, route_rows, route_scale, moe_gain, gate_up, down_proj, folded):
    tok_count, width = local.shape
    seq_count = lax.axis_size("seq")
    per_device = gate_up.shape[0]
    own_experts = per_device // 2
    normed = rms_scale(local, moe_gain)
    named = route_rows[:, :, None] == jnp.arange(E, dtype=jnp.int32)[None, None, :]
    dense = jnp.sum(jnp.where(named, route_scale[:, :, None], 0.0), axis=1).astype(jnp.bfloat16)
    filler = jnp.zeros((tok_count, -(width + E) % 128), jnp.bfloat16)
    gathered = ring_gather(jnp.concatenate([normed, dense, filler], axis=1), folded, 0)
    rows = gathered[:, :, :width]
    scales = lax.dynamic_slice_in_dim(
        gathered[:, :, width : width + E], lax.axis_index("seq") * own_experts, own_experts, axis=2
    ).transpose(0, 2, 1)
    present = scales > 0
    before = (
        jnp.arange(tok_count, dtype=jnp.int32)[:, None]
        < jnp.arange(tok_count, dtype=jnp.int32)[None, :]
    ).astype(jnp.bfloat16)
    earlier = jnp.einsum(
        "neu,ut->net", present.astype(jnp.bfloat16), before, preferred_element_type=jnp.float32
    ).astype(jnp.int32)
    slot = jnp.where(present, earlier, -1)
    taken = slot[:, :, None, :] == jnp.arange(CAP, dtype=jnp.int32)[None, None, :, None]
    select = jnp.repeat(taken.astype(jnp.bfloat16), 2, axis=1)
    received = jnp.einsum(
        "npct,ntd->npcd", select, rows, preferred_element_type=jnp.float32
    ).astype(jnp.bfloat16)
    projected = jnp.einsum("spcd,pdh->spch", received, gate_up, preferred_element_type=jnp.float32)
    half = projected.shape[-1] // 2
    gate_part = projected[..., :half]
    up_part = projected[..., half:]
    hidden = (gate_part * jax.nn.sigmoid(1.702 * gate_part) * (up_part + 1.0)).astype(jnp.bfloat16)
    partial_value = jnp.einsum(
        "spch,phd->spcd", hidden, down_proj, preferred_element_type=jnp.float32
    )
    finished = (
        partial_value.reshape(seq_count, own_experts, 2, CAP, width)
        .sum(axis=2)
        .astype(jnp.bfloat16)
        .reshape(seq_count, own_experts * CAP, width)
    )
    combine = jnp.where(taken, scales[:, :, None, :], 0).astype(jnp.bfloat16)
    parts = jnp.einsum(
        "nkt,nkd->ntd",
        combine.reshape(seq_count, own_experts * CAP, tok_count),
        finished,
        preferred_element_type=jnp.float32,
    ).astype(jnp.bfloat16)
    weighted = ring_scatter(parts, folded, 1)
    return (local.astype(jnp.float32) + weighted).astype(jnp.bfloat16)


def split_body(
    folded,
    tokens,
    routes,
    route_weights,
    moe_gain,
    gate_up,
    down_proj,
    attn_gain,
    qkv_proj,
    head_sink_logits,
    out_proj,
):
    seq_count = lax.axis_size("seq")
    seq_index = lax.axis_index("seq")
    pipe_index = lax.axis_index("pipe")
    query_width = QUERY_HEADS * HEAD_SIZE
    kv_width = KEY_VALUE_HEADS * HEAD_SIZE
    share = out_proj.shape[0] // 2
    own_heads = QUERY_HEADS // 2
    query_part = lax.dynamic_index_in_dim(
        qkv_proj[:, :query_width].reshape(qkv_proj.shape[0], seq_count, 2, share),
        pipe_index,
        axis=2,
        keepdims=False,
    ).reshape(qkv_proj.shape[0], query_width // 2)
    qkv_part = jnp.concatenate([query_part, qkv_proj[:, query_width:]], axis=1)
    shard_rows = qkv_part.shape[0]
    padding = -shard_rows % 16
    qkv_part = jnp.pad(qkv_part, ((0, padding), (0, 0)))
    out_part = lax.dynamic_slice_in_dim(out_proj, pipe_index * share, share, axis=0)
    qkv_whole = lax.all_gather(qkv_part, "seq", axis=0, tiled=True)
    out_whole = lax.all_gather(out_part, "seq", axis=0, tiled=True)
    sinks = lax.dynamic_index_in_dim(
        head_sink_logits.reshape(seq_count, 2, share // HEAD_SIZE),
        pipe_index,
        axis=1,
        keepdims=False,
    ).reshape(KEY_VALUE_HEADS, own_heads // KEY_VALUE_HEADS, 1, 1)

    hidden = experts_by_rings(
        tokens[0], routes[0], route_weights[0], moe_gain, gate_up, down_proj, folded
    )
    tok_count, width = hidden.shape
    normed = rms_scale(hidden, attn_gain)
    other = exchanged(normed)
    first = pipe_index == 0
    both = jnp.concatenate(
        [jnp.where(first, normed, other), jnp.where(first, other, normed)], axis=0
    )
    spread = jnp.pad(
        both.reshape(2 * tok_count, seq_count, shard_rows), ((0, 0), (0, 0), (0, padding))
    ).reshape(2 * tok_count, seq_count * (shard_rows + padding))
    packed = jnp.dot(spread, qkv_whole, preferred_element_type=jnp.float32).astype(jnp.bfloat16)
    packed = packed.reshape(2, tok_count, query_width // 2 + 2 * kv_width)
    pairs = packed[:, :, query_width // 2 :]
    from_left = shifted(pairs[:, tok_count - WINDOW_SPAN :], "seq", 1)
    halo = jnp.where(seq_index == 0, from_left[:1], from_left)
    extended = jnp.concatenate([halo, pairs], axis=1)
    keys = extended[:, :, :kv_width].reshape(2, -1, KEY_VALUE_HEADS, HEAD_SIZE)
    values = extended[:, :, kv_width:].reshape(2, -1, KEY_VALUE_HEADS, HEAD_SIZE)
    queries = packed[:, :, : query_width // 2].reshape(
        2, tok_count, KEY_VALUE_HEADS, own_heads // KEY_VALUE_HEADS, HEAD_SIZE
    )
    scores = jnp.einsum(
        "mqhgd,mkhd->mhgqk", queries, keys, preferred_element_type=jnp.float32
    ) * (float(HEAD_SIZE) ** (-0.5))
    query_pos = jnp.arange(tok_count, dtype=jnp.int32)[:, None] + WINDOW_SPAN
    key_pos = jnp.arange(tok_count + WINDOW_SPAN, dtype=jnp.int32)[None, :]
    distance = query_pos - key_pos
    inside = (distance >= 0) & (distance < WINDOW_SPAN)
    known = (jnp.arange(2, dtype=jnp.int32) > 0) | (seq_index > 0)
    allowed = inside[None] & ((key_pos >= WINDOW_SPAN)[None] | known[:, None, None])
    weights = jnp.where(allowed[:, None, None], jnp.exp(scores), 0.0)
    probs = (weights / (jnp.sum(weights, axis=-1, keepdims=True) + jnp.exp(sinks))).astype(
        jnp.bfloat16
    )
    mixed = jnp.einsum("mhgqk,mkhd->mqhgd", probs, values, preferred_element_type=jnp.float32)
    attended = mixed.astype(jnp.bfloat16).reshape(2 * tok_count, query_width // 2)
    projected = jnp.dot(attended, out_whole, preferred_element_type=jnp.float32)
    early, late = projected[:tok_count], projected[tok_count:]
    given = jnp.where(first, late, early).astype(jnp.bfloat16)
    kept = jnp.where(first, early, late)
    total = kept + exchanged(given).astype(jnp.float32)
    return (hidden.astype(jnp.float32) + total).astype(jnp.bfloat16)[None]


def solution(mesh):
    in_specs = (
        P("pipe", ("groups", "seq"), None),
        P("pipe", ("groups", "seq"), None),
        P("pipe", ("groups", "seq"), None),
        P(),
        P("seq", None, None),
        P("seq", None, None),
        P(),
        P("seq", None),
        P(),
        P("seq", None),
    )
    out_specs = P("pipe", ("groups", "seq"), None)
    seq_count, pipe_count = mesh.shape["seq"], mesh.shape["pipe"]
    split = (
        pipe_count == 2
        and seq_count % 2 == 0
        and 2 * E // seq_count >= 2
        and QUERY_HEADS % (2 * seq_count) == 0
    )
    chosen = functools.partial(split_body, True) if split else body
    return jax.shard_map(
        chosen, mesh=mesh, in_specs=in_specs, out_specs=out_specs, check_vma=False
    )
```

profile of v0, /device:TPU:0, one launch (start us, length us, event | category | flops | bytes accessed | tf_op | source)
XLA Modules:
  0.0 218.7 jit_solution(7429652796593455654)
XLA Ops:
  6.5 1.3 slice.43
  7.9 0.4 reshape.158
  8.3 2.2 %dynamic-slice_reduce_fusion = bf16[180,8,128]{2,1,0:T(8,128)(2,1)S(1)} fusion(bf16[180,8,2,128]{3,2,1,0:T(2,128)(2,1)S(1)} %reshape.158, s32[]{:T(128)S(6)} %select_n.67), kind=kLoop, calls=%fused_computation.42 | loop fusion | bytes 737284 | tf_op jit(solution)/shard_map/jit(dynamic_index_in_dim)/dynamic_slice | solution.py:354
  10.6 0.9 fusion.38
  11.6 0.8 constant_dynamic-slice_fusion
  13.1 0.9 concatenate.12.own_ref
  13.9 62.4 %shard_map.100 = bf16[8,128,1536]{2,1,0:T(8,128)(2,1)} custom-call(bf16[128,1536]{1,0:T(8,128)(2,1)} %concatenate.12.own_ref), custom_call_target="tpu_custom_call" | custom-call | tf_op jit(solution)/shard_map/pallas_call | solution.py:223
  76.3 1.9 slice.39
  78.3 1.9 broadcast_compare_fusion
  80.2 1.1 copy.107
  81.4 1.0 copy.108
  82.4 2.0 convert_select_fusion
  84.4 1.2 copy.109
  85.6 1.1 copy.110
  86.7 0.6 eq.51
  87.3 0.7 eq.52
  88.1 0.8 broadcast_in_dim.89
  88.9 14.7 %fusion.4 = f32[8,4,48,1440]{3,2,0,1:T(8,128)} fusion(bf16[4,1440,1440]{2,1,0:T(8,128)(2,1)} %param.14, bf16[8,4,48,128]{3,2,0,1:T(8,128)(2,1)} %bitcast.109, bf16[8,128,1536]{2,1,0:T(8,128)(2,1)S(1)} %copy-done.2), kind=kOutput, calls=%fused_computation.5 | convolution fusion | flops 6938542080 | bytes 28975104 | tf_op jit(solution)/shard_map/spcd,pdh->spch/dot_general | solution.py:309
  103.7 10.7 %bitcast_reduce_fusion = bf16[8,2,48,1440]{3,2,0,1:T(8,128)(2,1)S(1)} fusion(bf16[4,720,1440]{2,1,0:T(8,128)(2,1)} %param.15, f32[8,4,48,1440]{3,2,0,1:T(8,128)} %fusion.4), kind=kOutput, calls=%fused_computation.2 | convolution fusion | flops 3195002880 | bytes 19353600 | tf_op jit(solution)/shard_map/spch,phd->spcd/dot_general | solution.py:314
  114.7 2.7 %convolution_convert_fusion = bf16[8,128,1440]{1,2,0:T(8,128)(2,1)} fusion(bf16[8,96,128]{2,1,0:T(8,128)(2,1)S(1)} %fusion.44, bf16[8,96,1440]{2,1,0:T(8,128)(2,1)S(1)} %bitcast.101), kind=kOutput, calls=%fused_computation.12 | convolution fusion | flops 284590080 | bytes 5357568 | tf_op jit(solution)/shard_map/nkt,nkd->ntd/dot_general | solution.py:324
  117.4 3.2 %copy.114.part_ref = bf16[8,128,1440]{2,1,0:T(8,128)(2,1)S(1)} copy(bf16[8,128,1440]{1,2,0:T(8,128)(2,1)} %convolution_convert_fusion) | data formatting | bytes 5898240 | tf_op jit(solution)/shard_map/convert_element_type | solution.py:329
  120.6 60.0 %shard_map.101 = f32[128,1440]{1,0:T(8,128)S(1)} custom-call(bf16[8,128,1440]{2,1,0:T(8,128)(2,1)S(1)} %copy.114.part_ref), custom_call_target="tpu_custom_call" | custom-call | tf_op jit(solution)/shard_map/pallas_call | solution.py:268
  181.1 1.6 collective-permute-done
  183.6 3.7 %convolution_convert_fusion.1 = bf16[256,1536]{1,0:T(8,128)(2,1)S(1)} fusion(bf16[256,1536]{0,1:T(8,128)(2,1)S(1)} %bitcast.106, bf16[1536,1536]{1,0:T(8,128)(2,1)} %all-gather.3.cloned.1.call-done), kind=kOutput, calls=%fused_computation.17 | convolution fusion | flops 1208352768 | bytes 6291456 | tf_op jit(solution)/shard_map/dot_general | solution.py:387
  187.4 1.0 collective-permute-start.1
  189.1 13.6 %collective-permute-done.1 = bf16[2,128,512]{2,1,0:T(8,128)(2,1)S(1)} collective-permute-done((bf16[2,128,512]{2,1,0:T(8,128)(2,1)S(1)}, bf16[2,128,512]{2,1,0:T(8,128)(2,1)S(1)}, u32[]{:S(2)}, u32[]{:S(2)}) %collective-permute-start.1) | collective-permute-done | bytes 262176 | tf_op jit(solution)/shard_map/ppermute | solution.py:31
  203.1 1.1 fusion.10
  204.3 1.1 fusion.27
  205.3 0.5 copy.121
  205.9 2.9 %fusion.39 = f32[256,1440]{1,0:T(8,128)S(1)} fusion(bf16[1024,1440]{0,1:T(8,128)(2,1)} %all-gather.5.cloned.1.call-done, bf16[128,8,2,128]{3,2,1,0:T(2,128)(2,1)S(1)} %bitcast.108), kind=kOutput, calls=%fused_computation.44 | convolution fusion | flops 754974720 | bytes 4947968 | tf_op jit(solution)/shard_map/dot_general | solution.py:413
  209.0 1.7 collective-permute-done.2
  210.9 0.9 copy.124
  (70 shorter events, 4.2 us)
Async XLA Ops:
  6.5 5.0 %copy-start = (bf16[256,1440]{0,1:T(8,128)(2,1)S(1)}, bf16[256,1440]{0,1:T(8,128)(2,1)}, u32[]{:S(2)}) copy-start(bf16[256,1440]{0,1:T(8,128)(2,1)} %param.19) | copy-start | bytes 2211844
  6.5 4.0 %slice-start = ((bf16[180,2560]{1,0:T(8,128)(2,1)}), bf16[180,512]{1,0:T(8,128)(2,1)S(1)}, s32[]{:S(2)}) async-start(bf16[180,2560]{1,0:T(8,128)(2,1)} %param.17), calls=%async_computation.2 | async-start | bytes 376832 | tf_op jit(solution)/shard_map/slice | solution.py:360
  6.5 177.0 %all-gather.3.cloned.1.call-start = ((), (), s32[]{:S(2)}) async-start(), calls=%async_computation | async-start | bytes 5308416 | tf_op jit(solution)/shard_map/all_gather | solution.py:365
  6.5 5.8 %copy-start.3 = (bf16[1,128,1440]{1,2,0:T(8,128)(2,1)S(1)}, bf16[1,128,1440]{1,2,0:T(8,128)(2,1)}, u32[]{:S(2)}) copy-start(bf16[1,128,1440]{1,2,0:T(8,128)(2,1)} %param.10) | copy-start | bytes 1105924
  7.8 4.9 %copy-start.6 = (f32[1,128,4]{1,2,0:T(4,128)S(1)}, f32[1,128,4]{1,2,0:T(4,128)}, u32[]{:S(2)}) copy-start(f32[1,128,4]{1,2,0:T(4,128)} %param.12) | copy-start | bytes 6148
  7.9 4.9 %copy-start.7 = (s32[1,128,4]{1,2,0:T(4,128)S(1)}, s32[1,128,4]{1,2,0:T(4,128)}, u32[]{:S(2)}) copy-start(s32[1,128,4]{1,2,0:T(4,128)} %param.11) | copy-start | bytes 6148
  7.9 5.0 %copy-start.5 = (f32[1440]{0:T(1024)S(1)}, f32[1440]{0:T(1024)}, u32[]{:S(2)}) copy-start(f32[1440]{0:T(1024)} %param.13) | copy-start | bytes 17284
  11.5 194.4 %all-gather.5.cloned.1.call-start = ((), (), s32[]{:S(2)}) async-start(), calls=%async_computation.1 | async-start | bytes 3317760 | tf_op jit(solution)/shard_map/all_gather | solution.py:366
  76.3 12.6 %copy-start.2 = (bf16[8,128,1536]{2,1,0:T(8,128)(2,1)S(1)}, bf16[8,128,1536]{2,1,0:T(8,128)(2,1)}, u32[]{:S(2)}) copy-start(bf16[8,128,1536]{2,1,0:T(8,128)(2,1)} %shard_map.100) | copy-start | bytes 9437188
  120.5 60.2 %copy-start.4 = (f32[1440]{0:T(1024)S(1)}, f32[1440]{0:T(1024)}, u32[]{:S(2)}) copy-start(f32[1440]{0:T(1024)} %param.16) | copy-start | bytes 17284
  180.9 1.8 collective-permute-start
  183.6 4.8 %copy-start.8 = (f32[32]{0:T(128)S(1)}, f32[32]{0:T(128)}, u32[]{:S(2)}) copy-start(f32[32]{0:T(128)} %param.18) | copy-start | bytes 388
  187.4 15.4 %collective-permute-start.1 = (bf16[2,128,512]{2,1,0:T(8,128)(2,1)S(1)}, bf16[2,128,512]{2,1,0:T(8,128)(2,1)S(1)}, u32[]{:S(2)}, u32[]{:S(2)}) collective-permute-start(bf16[2,128,512]{2,1,0:T(8,128)(2,1)S(1)} %slice.54), channel_id=1, source_target_pairs={{0,2},{2,4},{4,6},{6,8},{8,10},{10,12},{12,14},{14,0},{1,3},{3,5},... | collective-permute-start | bytes 786440 | tf_op jit(solution)/shard_map/ppermute | solution.py:31
  205.9 5.9 %copy-start.1 = (bf16[256,1440]{0,1:T(8,128)(2,1)S(1)}, bf16[256,1440]{0,1:T(8,128)(2,1)}, u32[]{:S(2)}) copy-start(bf16[256,1440]{0,1:T(8,128)(2,1)} %param.19) | copy-start | bytes 2211844
  209.0 1.8 collective-permute-start.2
Sparse Core Ops, SparseCore 0:
  11.6 97.4 all-gather.2
  111.1 78.5 all-gather.4
where the time goes:
time: 219 us
  Pallas kernels  122 us (56%)
  matrix products  37.1 us (17%)
  local copies, waits for them, and re-layouts  20.6 us (9%)
  waiting for transfers between devices  17 us (8%)
  between operations  13.9 us (6%)
  other arithmetic  6.63 us (3%)
    pallas_call x1, Pallas kernels, ring_gather(): pl.pallas_call(functools.partial(gather_kernel, count, folded), out_shape...  62.4 us
    pallas_call x1, Pallas kernels, ring_scatter(): pl.pallas_call(functools.partial(scatter_kernel, count, folded), out_shap...  60 us
    dot_general x1, matrix products, experts_by_rings(): jnp.einsum('spcd,pdh->spch', received, gate_up, preferred_element_type=jn...  14.7 us
    ppermute x1, waiting for transfers between devices, shifted(): return lax.ppermute(value, axis, pairs)  13.6 us
    dot_general x1, matrix products, experts_by_rings(): jnp.einsum('spch,phd->spcd', hidden, down_proj, preferred_element_type=jn...  10.7 us
  transfers between devices with their start and end apart: 5, of which 3 were waited for; matrix products, arithmetic and copies ran while one was open for 25% of the time, Pallas kernels for 56%

commit v1 on v0

v1 whole, which is shorter than its diff:
```python
import functools

import jax
import jax.numpy as jnp
from jax import lax
from jax.experimental import pallas as pl
from jax.experimental.pallas import tpu as pltpu
from jax.sharding import PartitionSpec as P

MESH = pl.DeviceIdType.MESH
E = 16
TOP = 4
QUERY_HEADS = 32
KEY_VALUE_HEADS = 4
HEAD_SIZE = 64
WINDOW_SPAN = 128
HALF = 720
CAP = 48


eps = 1e-05


def from_partner(value, axis, distance):
    return lax.ppermute(value, axis, [(i, i ^ 1 << distance) for i in range(lax.axis_size(axis))])


def shifted(value, axis, steps):
    count = lax.axis_size(axis)
    pairs = [(source, (source + steps) % count) for source in range(count)]
    return lax.ppermute(value, axis, pairs)


def passed_along(value, axis, steps):
    count = lax.axis_size(axis)
    first, last = (max(0, -steps), min(count, count - steps))
    return lax.ppermute(value, axis, [(source, source + steps) for source in range(first, last)])


def rms_scale(value_matrix, gain):
    widened = value_matrix.astype(jnp.float32)
    mean_square = jnp.mean(widened * widened, axis=-1, keepdims=True)
    return (widened * lax.rsqrt(mean_square + eps) * gain).astype(jnp.bfloat16)


def slot_positions(route_rows):
    flat = route_rows.reshape(-1)
    onehot = (flat[:, None] == jnp.arange(E, dtype=jnp.int32)[None, :]).astype(jnp.int32)
    earlier = jnp.cumsum(onehot, axis=0) - onehot
    return flat * CAP + jnp.sum(earlier * onehot, axis=1)


def expert_layer(local, route_rows, route_scale, moe_gain, gate_up, down_proj):
    tok_count, width = local.shape
    seq_count = lax.axis_size("seq")
    per_device = gate_up.shape[0]
    normed = rms_scale(local, moe_gain)
    positions = slot_positions(route_rows)
    select = (positions[None, :] == jnp.arange(E * CAP, dtype=jnp.int32)[:, None]).astype(
        jnp.bfloat16
    )
    repeated = jnp.repeat(normed, TOP, axis=0)
    table = jnp.dot(select, repeated, preferred_element_type=jnp.float32).astype(jnp.bfloat16)
    by_expert = table.reshape(E, CAP, width)
    first = lax.axis_index("seq") % 2 == 0
    outgoing = jnp.repeat(by_expert, 2, axis=0).reshape(seq_count, per_device, CAP, width)
    received = lax.all_to_all(outgoing, "seq", split_axis=0, concat_axis=0, tiled=True)
    projected = jnp.einsum("spcd,pdh->spch", received, gate_up, preferred_element_type=jnp.float32)
    gate_part = projected[..., :HALF]
    up_part = projected[..., HALF:]
    hidden = (gate_part * jax.nn.sigmoid(1.702 * gate_part) * (up_part + 1.0)).astype(jnp.bfloat16)
    partial_value = jnp.einsum(
        "spch,phd->spcd", hidden, down_proj, preferred_element_type=jnp.float32
    )
    if per_device >= 2:
        finished = (
            partial_value.reshape(seq_count, per_device // 2, 2, CAP, width)
            .sum(axis=2)
            .astype(jnp.bfloat16)
        )
    else:
        lower_rows = partial_value[:, :, : CAP // 2]
        upper_rows = partial_value[:, :, CAP // 2 :]
        kept = jnp.where(first, lower_rows, upper_rows)
        given = jnp.where(first, upper_rows, lower_rows)
        partner_part = from_partner(given.astype(jnp.bfloat16), "seq", 0).astype(given.dtype)
        finished = (kept + partner_part).astype(jnp.bfloat16)
    summed = lax.all_to_all(finished, "seq", split_axis=0, concat_axis=0, tiled=True).reshape(
        E * CAP, width
    )
    picked = lax.dot_general(
        select, summed, (((0,), (0,)), ((), ())), preferred_element_type=jnp.float32
    )
    weighted = jnp.sum(picked.reshape(tok_count, TOP, width) * route_scale[:, :, None], axis=1)
    return (local.astype(jnp.float32) + weighted).astype(jnp.bfloat16)


def attend(query_matrix, keys_extended, values_extended, head_sink_logits, halo_valid):
    tok_count = query_matrix.shape[0]
    query_groups = QUERY_HEADS // KEY_VALUE_HEADS
    attention_block = min(tok_count, 512)
    scale = float(HEAD_SIZE) ** (-0.5)
    sink_mass_total = jnp.exp(head_sink_logits).reshape(KEY_VALUE_HEADS, query_groups, 1, 1)
    block_queries = query_matrix.reshape(attention_block, KEY_VALUE_HEADS, query_groups, HEAD_SIZE)
    block_keys = keys_extended.reshape(attention_block + WINDOW_SPAN, KEY_VALUE_HEADS, HEAD_SIZE)
    block_values = values_extended.reshape(
        attention_block + WINDOW_SPAN, KEY_VALUE_HEADS, HEAD_SIZE
    )
    scores = (
        jnp.einsum("qhgd,khd->hgqk", block_queries, block_keys, preferred_element_type=jnp.float32)
        * scale
    )
    query_pos = jnp.arange(attention_block, dtype=jnp.int32)[:, None] + WINDOW_SPAN
    key_pos = jnp.arange(attention_block + WINDOW_SPAN, dtype=jnp.int32)[None, :]
    distance = query_pos - key_pos
    allowed = (
        (distance >= 0) & (distance < WINDOW_SPAN) & ((key_pos + 0 >= WINDOW_SPAN) | halo_valid)
    )
    weights = jnp.where(allowed, jnp.exp(scores), 0.0)
    probs = (weights / (jnp.sum(weights, axis=-1, keepdims=True) + sink_mass_total)).astype(
        jnp.bfloat16
    )
    mixed = jnp.einsum("hgqk,khd->qhgd", probs, block_values, preferred_element_type=jnp.float32)
    outputs = mixed.reshape(attention_block, QUERY_HEADS * HEAD_SIZE).astype(jnp.bfloat16)
    return outputs


def body(
    tokens,
    routes,
    route_weights,
    moe_gain,
    gate_up,
    down_proj,
    attn_gain,
    qkv_proj,
    head_sink_logits,
    out_proj,
):
    hidden = expert_layer(tokens[0], routes[0], route_weights[0], moe_gain, gate_up, down_proj)
    tok_count, width = hidden.shape
    normed = rms_scale(hidden, attn_gain)
    seq_index = lax.axis_index("seq")
    pipe_index = lax.axis_index("pipe")
    halo_valid = (seq_index > 0) | (pipe_index > 0)
    query_width = QUERY_HEADS * HEAD_SIZE
    width_of_pair = KEY_VALUE_HEADS * HEAD_SIZE
    columns = normed
    packed_heads = jnp.dot(
        columns,
        lax.all_gather(qkv_proj, "seq", axis=0, tiled=True),
        preferred_element_type=jnp.float32,
    ).astype(jnp.bfloat16)
    from_left = shifted(packed_heads[tok_count - WINDOW_SPAN :, query_width:], "seq", 1)
    from_section = passed_along(from_left, "pipe", 1)
    halo_pairs = jnp.where(seq_index == 0, from_section, from_left)
    query_matrix = packed_heads[:, :query_width]
    pairs_ext = jnp.concatenate([halo_pairs, packed_heads[:, query_width:]], axis=0)
    keys_extended = pairs_ext[:, :width_of_pair]
    values_extended = pairs_ext[:, width_of_pair:]
    attended = attend(query_matrix, keys_extended, values_extended, head_sink_logits, halo_valid)
    columns = attended
    projected = jnp.dot(
        columns,
        lax.all_gather(out_proj, "seq", axis=0, tiled=True),
        preferred_element_type=jnp.float32,
    )
    return (hidden.astype(jnp.float32) + projected).astype(jnp.bfloat16)[None]


def ring_place(index, count, folded):
    if not folded:
        return index
    line, side = index // 2, index % 2
    return line + side * (count - 1 - 2 * line)

def ring_index(place, count, folded):
    if not folded:
        return place
    side = place // (count // 2)
    line = place + side * (count - 1 - 2 * place)
    return 2 * line + side


def copy_to(src, dst, send, recv, **device):
    return pltpu.make_async_remote_copy(src_ref=src, dst_ref=dst, send_sem=send, recv_sem=recv,
        device_id=device, device_id_type=MESH)


def dot(a, b, dims=((1,), (0,))):
    return lax.dot_general(a, b, (dims, ((), ())), preferred_element_type=jnp.float32)


def layer_kernel(
    tok_t_ref, tok_ref, routes_ref, weights_ref, gain_ref, attn_gain_ref, sink_ref,
    gate_up_ref, down_ref, qkv_ref, out_t_ref,
    out_ref,
    blocks, picked, combine, gu, dn, proj, act, done, parts, held, wq, wo,
    both, kv, halo, queries, mixed, given, back,
    gu_sem, dn_sem, wq_sem, wo_sem, ag_s, ag_r, rs_s, rs_r, q_s, q_r, qx_s, qx_r,
    o_s, o_r, ox_s, ox_r, pair_s, pair_r, halo_s, halo_r,
):
    count = lax.axis_size("seq")
    steps = count // 2
    me = lax.axis_index("seq")
    core = lax.axis_index("pipe")
    group = lax.axis_index("groups")
    width, tok_count = tok_t_ref.shape
    own = picked.shape[0]
    slots = own * CAP
    place = ring_place(me, count, True)
    at = lambda offset: ring_index(lax.rem(place + offset + count, count), count, True)
    peers = (at(1), at(-1))
    following, preceding = lax.rem(me + 1, count), lax.rem(me + count - 1, count)
    other_core, other_group = 1 - core, 1 - group
    sends = []

    def launch(copy):
        copy.start()
        sends.append((None, copy))
        return copy

    qw, kw = queries.shape[2], kv.shape[2] // 2
    all_q = QUERY_HEADS * HEAD_SIZE
    all_k = KEY_VALUE_HEADS * HEAD_SIZE
    wo_slot = lax.rem(me, steps)
    holds = lambda origin: lax.div(origin, steps) == core
    wo_copy = pltpu.make_async_copy(out_t_ref, wo.at[wo_slot], wo_sem.at[0])

    @pl.when(holds(me))
    def _():
        wo_copy.start()

    wq_copies = []
    for i, (source, goal, size) in enumerate((
        (all_q + core * kw, 0, kw), (all_q + all_k + core * kw, kw, kw), (core * qw, 2 * kw, qw))):
        wq_copies.append(pltpu.make_async_copy(
            qkv_ref.at[:, pl.ds(pl.multiple_of(source, 128), size)],
            wq.at[me, :, pl.ds(goal, size)], wq_sem.at[i]))
    for copy in wq_copies:
        copy.start()
    gu_copies = [pltpu.make_async_copy(gate_up_ref.at[j], gu.at[j], gu_sem.at[j]) for j in range(2 * own)]
    dn_copies = [pltpu.make_async_copy(down_ref.at[j], dn.at[j], dn_sem.at[j]) for j in range(2 * own)]
    for copy in gu_copies + dn_copies:
        copy.start()

    tall = tok_t_ref[...].astype(jnp.float32)
    scale = lax.rsqrt(jnp.sum(tall * tall, axis=0, keepdims=True) / width + eps)
    for i in range(0, width, 128):
        size = min(128, width - i)
        blocks[me, i : i + size, :] = (
            tok_t_ref[i : i + size, :].astype(jnp.float32) * scale * gain_ref[:size, i // 128 : i // 128 + 1]
        ).astype(jnp.bfloat16)
    expert_row = lax.broadcasted_iota(jnp.int32, (E, tok_count), 0)
    dense = jnp.zeros((E, tok_count), jnp.float32)
    for j in range(TOP):
        dense = dense + jnp.where(expert_row == routes_ref[j : j + 1, :], weights_ref[j : j + 1, :], 0.0)
    blocks[me, width : width + E, :] = dense.astype(jnp.bfloat16)

    barrier = pltpu.get_barrier_semaphore()
    for device in ({"seq": peers[0]}, {"seq": peers[1]}, {"seq": following}, {"seq": preceding},
                   {"pipe": other_core}, {"groups": other_group}):
        pl.semaphore_signal(barrier, inc=1, device_id=device, device_id_type=MESH)
    pl.semaphore_wait(barrier, 6)

    rows_all = blocks.shape[1]
    cut = (rows_all // 2 + 15) // 16 * 16
    pieces = (pl.ds(0, cut), pl.ds(cut, rows_all - cut))
    ag = {}

    def ag_send(way, step, piece):
        origin = at(-step if way == 0 else step)
        ref = blocks.at[origin, pieces[piece]]
        ag[way, step, piece] = launch(copy_to(ref, ref, ag_s.at[way, step, piece], ag_r.at[way, step, piece], seq=peers[way]))

    qcols = wq.shape[2] // 2
    qcut = (qcols // 2 + 127) // 128 * 128
    q = {}
    qx = {}

    def q_part(way, step):
        base = pl.multiple_of(group * qcols, 128)
        if step < steps - 1:
            return pl.ds(base, qcols)
        return pl.ds(base, qcut) if way == 0 else pl.ds(base + qcut, qcols - qcut)

    def q_send(way, step):
        ref = wq.at[at(-step if way == 0 else step), :, q_part(way, step)]
        q[way, step] = launch(copy_to(ref, ref, q_s.at[way, step], q_r.at[way, step], seq=peers[way]))

    def q_cross(way, step):
        q[way, step].wait_recv()
        ref = wq.at[at(-step - 1 if way == 0 else step + 1), :, q_part(way, step)]
        qx[way, step] = launch(copy_to(ref, ref, qx_s.at[way, step], qx_r.at[way, step], groups=other_group))

    def q_begin():
        for copy in wq_copies:
            copy.wait()
        for way in (0, 1):
            q_send(way, 0)

    def q_step(step):
        for way in (0, 1):
            q_cross(way, step - 1)
            if step < steps:
                q_send(way, step)

    orows = wo.shape[1] // 2
    ocut = (orows // 2 + 15) // 16 * 16
    o_sends = []

    def o_part(way, step):
        base = pl.multiple_of(group * orows, 16)
        if step < steps - 1:
            return pl.ds(base, orows)
        return pl.ds(base, ocut) if way == 0 else pl.ds(pl.multiple_of(base + ocut, 16), orows - ocut)

    def o_copy(way, step):
        origin = at(-step if way == 0 else step)
        ref = wo.at[lax.rem(origin, steps), o_part(way, step)]
        return holds(origin), copy_to(ref, ref, o_s.at[way, step], o_r.at[way, step], seq=peers[way])

    def o_landed(way, step):
        origin = at(-step - 1 if way == 0 else step + 1)
        ref = wo.at[lax.rem(origin, steps), o_part(way, step)]
        return (holds(origin), copy_to(ref, ref, o_s.at[way, step], o_r.at[way, step], seq=peers[way]),
                copy_to(ref, ref, ox_s.at[way, step], ox_r.at[way, step], groups=other_group))

    def o_begin():
        @pl.when(holds(me))
        def _():
            wo_copy.wait()
        for way in (0, 1):
            cond, copy = o_copy(way, 0)

            @pl.when(cond)
            def _():
                copy.start()
            o_sends.append((cond, copy))

    def o_step(step):
        for way in (0, 1):
            cond, arrived, crossing = o_landed(way, step - 1)

            @pl.when(cond)
            def _():
                arrived.wait_recv()
                crossing.start()
            o_sends.append((cond, crossing))
            if step < steps:
                onward, copy = o_copy(way, step)

                @pl.when(onward)
                def _():
                    copy.start()
                o_sends.append((onward, copy))

    lane_tok = lax.broadcasted_iota(jnp.int32, (tok_count, tok_count), 1)
    row_tok = lax.broadcasted_iota(jnp.int32, (tok_count, tok_count), 0)
    before = jnp.where(row_tok < lane_tok, 1.0, 0.0).astype(jnp.bfloat16)
    slot_row = lax.broadcasted_iota(jnp.int32, (tok_count, tok_count), 0).astype(jnp.float32)

    def process(n):
        table = blocks[n, width : width + E, :].astype(jnp.float32)
        present = table > 0.0
        earlier = dot(jnp.where(present, 1.0, 0.0).astype(jnp.bfloat16), before)
        slot = jnp.where(present, earlier, -1.0)
        comb = jnp.zeros((tok_count, tok_count), jnp.float32)
        for e in range(own):
            mine = expert_row == me * own + e
            slot_e = jnp.sum(jnp.where(mine, slot, 0.0), axis=0, keepdims=True)
            scale_e = jnp.sum(jnp.where(mine, table, 0.0), axis=0, keepdims=True)
            hit = (slot_row == slot_e + float(e * CAP)) & (slot_e >= 0.0)
            comb = jnp.where(hit, scale_e, comb)
        combine[n] = comb.T.astype(jnp.bfloat16)
        select = jnp.where(comb > 0.0, 1.0, 0.0).astype(jnp.bfloat16)[:slots]
        rows = dot(select, blocks[n, :width, :], ((1,), (1,))).astype(jnp.bfloat16)
        for e in range(own):
            picked[e, n] = rows[e * CAP : (e + 1) * CAP]

    for piece in (0, 1):
        for way in (0, 1):
            ag_send(way, 0, piece ^ way)
    o_begin()
    process(me)
    for step in range(1, steps):
        for piece in (0, 1):
            for way in (0, 1):
                ag[way, step - 1, piece ^ way].wait_recv()
                if step < steps - 1 or piece == 0:
                    ag_send(way, step, piece ^ way)
        o_step(step)
        process(at(-step))
        process(at(step))
    ag[0, steps - 1, 0].wait_recv()
    ag[1, steps - 1, 1].wait_recv()
    process(at(steps))
    o_step(steps)

    q_begin()
    pos = {0: 1, 1: 2, 2: 3, 3: 4}
    half = dn.shape[1]
    chunk = CAP
    for e in range(own):
        for j in (2 * e, 2 * e + 1):
            gu_copies[j].wait()
            x = picked[e].reshape(count * CAP, width)
            proj[...] = dot(x, gu[j])

            @pl.loop(0, count)
            def _(i):
                r = pl.ds(pl.multiple_of(i * chunk, 16), chunk)
                gate = proj[r, :half]
                up = proj[r, half:]
                act[j % 2, r, :] = (gate * jax.nn.sigmoid(1.702 * gate) * (up + 1.0)).astype(jnp.bfloat16)

            if j < steps:
                q_step(j + 1)
        dn_copies[2 * e].wait()
        dn_copies[2 * e + 1].wait()
        result = dot(act[0], dn[2 * e]) + dot(act[1], dn[2 * e + 1])
        done[:, e * CAP : (e + 1) * CAP, :] = result.astype(jnp.bfloat16).reshape(count, CAP, width)
    for step in range(2 * own + 1, steps + 1):
        q_step(step)

    def part(n):
        parts[n] = dot(combine[n][:, :slots], done[n]).astype(jnp.bfloat16)

    hrows = tok_count // 2
    lanes = [pl.ds(0, hrows), pl.ds(hrows, hrows)]
    rs = {}

    def rs_send(way, step, piece):
        goal = at((steps - step) * (1 if way == 0 else -1))
        here = lanes[piece]
        if (way, step - 1, piece) in rs:
            rs[way, step - 1, piece].wait_recv()
            held[way, step - 1, here] = (
                held[way, step - 1, here].astype(jnp.float32) + parts[goal, here].astype(jnp.float32)
            ).astype(jnp.bfloat16)
            src = held.at[way, step - 1, here]
        else:
            src = parts.at[goal, here]
        rs[way, step, piece] = launch(copy_to(src, held.at[way, step, here], rs_s.at[way, step, piece], rs_r.at[way, step, piece], seq=peers[way]))

    part(at(steps))
    rs_send(0, 0, 0)
    rs_send(1, 0, 1)
    for way in (0, 1):
        part(at((steps - 1) * (1 if way == 0 else -1)))
        rs_send(way, 1, 1 - way)
    for offset in range(steps - 2, 0, -1):
        part(at(offset))
        part(at(-offset))
    part(me)
    rs_send(0, 1, 0)
    rs_send(1, 1, 1)
    for step in range(2, steps):
        for piece in (0, 1):
            for way in (0, 1):
                rs_send(way, step, 1 ^ piece ^ way)
    for piece in (0, 1):
        for way in (0, 1):
            rs[way, steps - 1, piece].wait_recv()
    summed = (tok_ref[...].astype(jnp.float32) + parts[me].astype(jnp.float32)
        + held[0, steps - 1].astype(jnp.float32) + held[1, steps - 1].astype(jnp.float32)).astype(jnp.bfloat16)
    hidden = summed.astype(jnp.float32)
    scale = lax.rsqrt(jnp.sum(hidden * hidden, axis=1, keepdims=True) / width + eps)
    normed = hidden * scale * attn_gain_ref[...]
    shard = wq.shape[1]
    for i in range(count):
        both[core, i] = normed[:, i * shard : (i + 1) * shard].astype(jnp.bfloat16)
    pair = launch(copy_to(both.at[core], both.at[core], pair_s.at[0], pair_r.at[0], pipe=other_core))

    for key in qx:
        qx[key].wait_recv()
    pair.wait_recv()

    def project(columns):
        total = None
        for i in range(count):
            x = both[:, i].reshape(2 * tok_count, shard)
            term = dot(x, wq[i, :, columns])
            total = term if total is None else total + term
        return total.astype(jnp.bfloat16).reshape(2, tok_count, -1)

    kv[...] = project(pl.ds(0, 2 * kw))
    along = launch(copy_to(kv, halo, halo_s.at[0], halo_r.at[0], seq=following))
    queries[...] = project(pl.ds(2 * kw, qw))
    along.wait_recv()

    lane = lax.broadcasted_iota(jnp.int32, (tok_count, 2 * tok_count), 1)
    row = lax.broadcasted_iota(jnp.int32, (tok_count, 2 * tok_count), 0)
    left = lane < tok_count
    past = jnp.where(left, lane, lane - tok_count) > row
    low = lax.broadcasted_iota(jnp.int32, (tok_count, 2 * HEAD_SIZE), 1) < HEAD_SIZE

    def stacked(tile, head):
        tile = tile.astype(jnp.float32)
        kept = jnp.where(low if head == 0 else ~low, tile, 0.0)
        turned = pltpu.roll(kept, HEAD_SIZE, 1)
        pair_of = (kept, turned) if head == 0 else (turned, kept)
        return jnp.concatenate(pair_of, axis=0).astype(jnp.bfloat16)

    tiles = qw // 128
    per_head = tiles // 2
    for m in range(2):
        source = jnp.where(me == 0, 0, m)
        known = (me > 0) if m == 0 else (me >= 0)
        for head in range(2):
            k_own = stacked(kv[m, :, :kw], head)
            v_own = stacked(kv[m, :, kw:], head)
            k_past = stacked(halo[source, :, :kw], head)
            v_past = stacked(halo[source, :, kw:], head)
            for t in range(head * per_head, (head + 1) * per_head):
                x = queries[m, :, t * 128 : (t + 1) * 128]
                score = jnp.where(past, dot(x, k_past, ((1,), (1,))), dot(x, k_own, ((1,), (1,))))
                weight = jnp.exp(score * (float(HEAD_SIZE) ** -0.5))
                weight = jnp.where(past & jnp.logical_not(known), 0.0, weight)
                mass = jnp.where(left, jnp.sum(weight[:, :tok_count], axis=1, keepdims=True),
                    jnp.sum(weight[:, tok_count:], axis=1, keepdims=True)) + sink_ref[t : t + 1, :]
                probs = weight / mass
                mixed[m, :, t * 128 : (t + 1) * 128] = (
                    dot(jnp.where(past, 0.0, probs).astype(jnp.bfloat16), v_own)
                    + dot(jnp.where(past, probs, 0.0).astype(jnp.bfloat16), v_past)
                ).astype(jnp.bfloat16)

    for way in (0, 1):
        for step in range(steps):
            cond, _, crossing = o_landed(way, step)

            @pl.when(cond)
            def _():
                crossing.wait_recv()

    share = wo.shape[2]

    def output(m):
        total = None
        for i in range(steps):
            term = dot(mixed[m, :, i * share : (i + 1) * share], wo[i], ((1,), (1,)))
            total = term if total is None else total + term
        return total

    given[...] = output(other_core).astype(jnp.bfloat16)
    last = launch(copy_to(given, back, pair_s.at[1], pair_r.at[1], pipe=other_core))
    kept = output(core)
    last.wait_recv()
    out_ref[...] = (hidden + kept + back[...].astype(jnp.float32)).astype(jnp.bfloat16)
    for _, copy in sends:
        copy.wait_send()
    for cond, copy in o_sends:
        @pl.when(cond)
        def _():
            copy.wait_send()


def whole_layer(
    tokens, routes, route_weights, moe_gain, gate_up, down_proj, attn_gain, qkv_proj,
    head_sink_logits, out_proj,
):
    count = lax.axis_size("seq")
    core = lax.axis_index("pipe")
    steps = count // 2
    tok_count, width = tokens.shape[1:]
    own = gate_up.shape[0] // 2
    half = down_proj.shape[1]
    heads = QUERY_HEADS // 2
    qw = heads * HEAD_SIZE
    kw = KEY_VALUE_HEADS * HEAD_SIZE // 2
    tok = tokens[0]
    gain = jnp.pad(moe_gain, (0, -width % 128)).reshape(-1, 128).T
    sinks = jnp.exp(lax.dynamic_slice_in_dim(head_sink_logits, core * heads, heads))
    sinks = jnp.repeat(sinks.reshape(heads // 2, 2), tok_count, axis=1)
    dma = pltpu.SemaphoreType.DMA
    bf16 = jnp.bfloat16
    vm = pl.BlockSpec(memory_space=pltpu.VMEM)
    hbm = pl.BlockSpec(memory_space=pl.ANY)
    out = pl.pallas_call(
        layer_kernel,
        out_shape=jax.ShapeDtypeStruct((tok_count, width), bf16),
        in_specs=[vm] * 7 + [hbm] * 4,
        out_specs=vm,
        scratch_shapes=[
            pltpu.VMEM((count, width + E, tok_count), bf16),
            pltpu.VMEM((own, count, CAP, width), bf16),
            pltpu.VMEM((count, tok_count, tok_count), bf16),
            pltpu.VMEM(gate_up.shape, bf16),
            pltpu.VMEM(down_proj.shape, bf16),
            pltpu.VMEM((count * CAP, 2 * half), jnp.float32),
            pltpu.VMEM((2, count * CAP, half), bf16),
            pltpu.VMEM((count, own * CAP, width), bf16),
            pltpu.VMEM((count, tok_count, width), bf16),
            pltpu.VMEM((2, steps, tok_count, width), bf16),
            pltpu.VMEM((count, qkv_proj.shape[0], 2 * kw + qw), bf16),
            pltpu.VMEM((steps, width, out_proj.shape[0]), bf16),
            pltpu.VMEM((2, count, tok_count, qkv_proj.shape[0]), bf16),
            pltpu.VMEM((2, tok_count, 2 * kw), bf16),
            pltpu.VMEM((2, tok_count, 2 * kw), bf16),
            pltpu.VMEM((2, tok_count, qw), bf16),
            pltpu.VMEM((2, tok_count, qw), bf16),
            pltpu.VMEM((tok_count, width), bf16),
            pltpu.VMEM((tok_count, width), bf16),
            dma((2 * own,)), dma((2 * own,)), dma((3,)), dma((1,)),
            dma((2, steps, 2)), dma((2, steps, 2)), dma((2, steps, 2)), dma((2, steps, 2)),
            dma((2, steps)), dma((2, steps)), dma((2, steps)), dma((2, steps)),
            dma((2, steps)), dma((2, steps)), dma((2, steps)), dma((2, steps)),
            dma((2,)), dma((2,)), dma((1,)), dma((1,)),
        ],
        compiler_params=pltpu.CompilerParams(
            collective_id=0, has_side_effects=True, vmem_limit_bytes=67043328),
    )(tok.T, tok, routes[0].T, route_weights[0].T, gain, attn_gain[None], sinks,
      gate_up, down_proj, qkv_proj, out_proj.T)
    return out[None]


def solution(mesh):
    in_specs = (
        P("pipe", ("groups", "seq"), None),
        P("pipe", ("groups", "seq"), None),
        P("pipe", ("groups", "seq"), None),
        P(),
        P("seq", None, None),
        P("seq", None, None),
        P(),
        P("seq", None),
        P(),
        P("seq", None),
    )
    out_specs = P("pipe", ("groups", "seq"), None)
    seq_count, pipe_count, group_count = mesh.shape["seq"], mesh.shape["pipe"], mesh.shape["groups"]
    whole = (
        pipe_count == 2
        and group_count == 2
        and seq_count % 2 == 0
        and 2 * E // seq_count == 4
        and QUERY_HEADS % (2 * seq_count) == 0
    )
    return jax.shard_map(
        whole_layer if whole else body, mesh=mesh, in_specs=in_specs, out_specs=out_specs, check_vma=False
    )
```

time: 219 us -> 136 us (0.62)
  matrix products: 37.1 us -> 0 us
  waiting for transfers between devices: 17 us -> 0 us
  between operations: 13.9 us -> 0.01 us
  local copies, waits for them, and re-layouts: 20.6 us -> 8.11 us
  other arithmetic: 6.63 us -> 0 us
  Pallas kernels: 122 us -> 128 us
    dot_general x8 -> x0, matrix products: 37.1 us -> none  [the longest x1 14.7 us: experts_by_rings(): jnp.einsum('spcd,pdh->spch', received, gate_up, preferred_element_type=jn...]
    ppermute x3 -> x0, waiting for transfers between devices: 17 us -> none  [the longest x1 13.6 us: shifted(): return lax.ppermute(value, axis, pairs)]
    pallas_call x2 -> x1, Pallas kernels: 122 us -> 128 us  [whole_layer(): pl.pallas_call(layer_kernel, out_shape=jax.ShapeDtypeStruct((tok_count, w...]
    convert_element_type x5 -> x0, local copies, waits for them, and re-layouts: 4.05 us -> none  [the longest x1 3.18 us: experts_by_rings(): parts = jnp.einsum('nkt,nkd->ntd', combine.reshape(seq_count, own_experts...]
    slice x9 -> x0, local copies, waits for them, and re-layouts: 3.86 us -> none  [the longest x1 1.95 us: experts_by_rings(): gathered[:, :, width:width + E]]
    dynamic_slice x2 -> x0, local copies, waits for them, and re-layouts: 2.97 us -> none  [the longest x1 2.2 us: split_body(): lax.dynamic_index_in_dim(qkv_proj[:, :query_width].reshape(qkv_proj.shape...]
    select_n x4 -> x0, other arithmetic: 2.39 us -> none  [the longest x1 1.98 us: experts_by_rings(): slot = jnp.where(present, earlier, -1)]
  transfers between devices with their start and end apart: 5 -> 0, of which waited for: 3 -> 0; matrix products, arithmetic and copies ran while one was open for 25% -> 0% of each run, Pallas kernels for 56% -> 0%
where the time goes in v1:
time: 136 us
  Pallas kernels  128 us (94%)
  local copies, waits for them, and re-layouts  8.11 us (6%)
    pallas_call x1, Pallas kernels, whole_layer(): pl.pallas_call(layer_kernel, out_shape=jax.ShapeDtypeStruct((tok_count, w...  128 us

profile of v1, /device:TPU:0, one launch (start us, length us, event | category | flops | bytes accessed | tf_op | source)
XLA Modules:
  0.0 135.9 jit_solution(16905074319878914668)
XLA Ops:
  0.0 0.7 dynamic-slice_exponential_fusion
  0.7 0.1 reshape.10
  0.8 0.1 copy.17
  0.9 1.3 broadcast_in_dim.9.attn_gain_ref
  2.2 0.7 broadcast_bitcast_fusion.sink_ref
  2.9 0.7 pad_bitcast_fusion
  3.6 0.7 copy.16
  4.3 1.9 %copy.15 = bf16[1,128,1440]{2,1,0:T(8,128)(2,1)} copy(bf16[1,128,1440]{1,2,0:T(8,128)(2,1)} %param.10) | data formatting | bytes 737280 | tf_op args[0]
  6.2 127.8 %shard_map.100 = bf16[128,1440]{1,0:T(8,128)(2,1)} custom-call(bf16[1440,128]{1,0:T(8,128)(2,1)} %bitcast.18, bf16[128,1440]{1,0:T(8,128)(2,1)} %bitcast.17, s32[4,128]{1,0:T(4,128)} %bitcast.21, f32[4,128]{1,0:T(4,128)} %bitcast.22, f32[128,12]{1,0:T(8,128)} %bitcast.20, f32[1,1440]{1,0:T(1,128)} %broadcast_in_dim.9.attn_gain_ref, ...), custom_call_target="tpu_custom_call" | custom-call | tf_op jit(solution)/shard_map/pallas_call | solution.py:579
  134.0 1.9 %copy.19 = bf16[1,128,1440]{1,2,0:T(8,128)(2,1)} copy(bf16[1,128,1440]{2,1,0:T(8,128)(2,1)} %bitcast.16) | data formatting | bytes 737280 | tf_op jit(solution)/shard_map/broadcast_in_dim | solution.py:614

commit v2 on v1

--- a/solution.py
+++ b/solution.py
@@ -192,13 +192,13 @@
 
 
 def layer_kernel(
-    tok_t_ref, tok_ref, routes_ref, weights_ref, gain_ref, attn_gain_ref, sink_ref,
+    tok_t_ref, routes_ref, weights_ref, gain_ref, attn_gain_ref, sink_ref,
     gate_up_ref, down_ref, qkv_ref, out_t_ref,
     out_ref,
     blocks, picked, combine, gu, dn, proj, act, done, parts, held, wq, wo,
-    both, kv, halo, queries, mixed, given, back,
+    both, kv, halo, queries, mixed, given, back, hid, hid_t,
     gu_sem, dn_sem, wq_sem, wo_sem, ag_s, ag_r, rs_s, rs_r, q_s, q_r, qx_s, qx_r,
-    o_s, o_r, ox_s, ox_r, pair_s, pair_r, halo_s, halo_r,
+    o_s, o_r, ox_s, ox_r, late_s, late_r, pair_s, pair_r, halo_s, halo_r,
 ):
     count = lax.axis_size("seq")
     steps = count // 2
@@ -248,8 +248,9 @@
     scale = lax.rsqrt(jnp.sum(tall * tall, axis=0, keepdims=True) / width + eps)
     for i in range(0, width, 128):
         size = min(128, width - i)
+        gain = jnp.broadcast_to(gain_ref[pl.ds(i, size)].reshape(1, size), (tok_count, size)).T
         blocks[me, i : i + size, :] = (
-            tok_t_ref[i : i + size, :].astype(jnp.float32) * scale * gain_ref[:size, i // 128 : i // 128 + 1]
+            tok_t_ref[i : i + size, :].astype(jnp.float32) * scale * gain
         ).astype(jnp.bfloat16)
     expert_row = lax.broadcasted_iota(jnp.int32, (E, tok_count), 0)
     dense = jnp.zeros((E, tok_count), jnp.float32)
@@ -338,6 +339,8 @@
                 copy.start()
             o_sends.append((cond, copy))
 
+    near = steps // 2
+
     def o_step(step):
         for way in (0, 1):
             cond, arrived, crossing = o_landed(way, step - 1)
@@ -347,13 +350,47 @@
                 arrived.wait_recv()
                 crossing.start()
             o_sends.append((cond, crossing))
-            if step < steps:
+            if step < near:
                 onward, copy = o_copy(way, step)
 
                 @pl.when(onward)
                 def _():
                     copy.start()
                 o_sends.append((onward, copy))
+
+    def late_copy(way, step, piece):
+        origin = at(-step if way == 0 else step)
+        ref = wo.at[lax.rem(origin, steps), pl.ds(piece * orows, orows)]
+        index = 2 * (step - near) + (piece ^ way)
+        return holds(origin), copy_to(ref, ref, late_s.at[way, index], late_r.at[way, index], seq=peers[way])
+
+    def late_send(step, order):
+        for way in (0, 1):
+            cond, copy = late_copy(way, step, order ^ way)
+            if order == 0:
+                if step == near:
+                    _, _, before_it = o_landed(way, step - 1)
+                    before_it_wait = before_it.wait_recv
+                else:
+                    origin_cond, before_it = late_landed(way, step - 1, 0)
+                    before_it_wait = before_it.wait_recv
+
+                @pl.when(cond)
+                def _():
+                    before_it_wait()
+                    copy.start()
+            else:
+                @pl.when(cond)
+                def _():
+                    copy.start()
+            o_sends.append((cond, copy))
+
+    def late_landed(way, step, order):
+        origin = at(-step - 1 if way == 0 else step + 1)
+        piece = order ^ way
+        ref = wo.at[lax.rem(origin, steps), pl.ds(piece * orows, orows)]
+        index = 2 * (step - near) + order
+        return holds(origin), copy_to(ref, ref, late_s.at[way, index], late_r.at[way, index], seq=peers[way])
 
     lane_tok = lax.broadcasted_iota(jnp.int32, (tok_count, tok_count), 1)
     row_tok = lax.broadcasted_iota(jnp.int32, (tok_count, tok_count), 0)
@@ -383,19 +420,22 @@
             ag_send(way, 0, piece ^ way)
     o_begin()
     process(me)
+    for i in range(0, width, 128):
+        size = min(128, width - i)
+        hid[:, i : i + size] = tok_t_ref[i : i + size, :].astype(jnp.float32).T
     for step in range(1, steps):
         for piece in (0, 1):
             for way in (0, 1):
                 ag[way, step - 1, piece ^ way].wait_recv()
                 if step < steps - 1 or piece == 0:
                     ag_send(way, step, piece ^ way)
-        o_step(step)
+        if step <= near:
+            o_step(step)
         process(at(-step))
         process(at(step))
     ag[0, steps - 1, 0].wait_recv()
     ag[1, steps - 1, 1].wait_recv()
     process(at(steps))
-    o_step(steps)
 
     q_begin()
     pos = {0: 1, 1: 2, 2: 3, 3: 4}
@@ -423,25 +463,36 @@
     for step in range(2 * own + 1, steps + 1):
         q_step(step)
 
+    hrows = tok_count // 2
+    tail = width % 128
+    full = width - tail
+    folds = 128 // tail
+    trows = hrows // folds
+    base = hrows * (full // 128)
+
     def part(n):
-        parts[n] = dot(combine[n][:, :slots], done[n]).astype(jnp.bfloat16)
-
-    hrows = tok_count // 2
-    lanes = [pl.ds(0, hrows), pl.ds(hrows, hrows)]
+        value = dot(combine[n][:, :slots], done[n])
+        for c in (0, 1):
+            rows = value[c * hrows : (c + 1) * hrows]
+            for i in range(0, full, 128):
+                parts[n, c, i // 128 * hrows : (i // 128 + 1) * hrows, :] = rows[:, i : i + 128].astype(jnp.bfloat16)
+            parts[n, c, base : base + trows, :] = jnp.concatenate(
+                [rows[k * trows : (k + 1) * trows, full:] for k in range(folds)], axis=1
+            ).astype(jnp.bfloat16)
+
     rs = {}
 
     def rs_send(way, step, piece):
         goal = at((steps - step) * (1 if way == 0 else -1))
-        here = lanes[piece]
         if (way, step - 1, piece) in rs:
             rs[way, step - 1, piece].wait_recv()
-            held[way, step - 1, here] = (
-                held[way, step - 1, here].astype(jnp.float32) + parts[goal, here].astype(jnp.float32)
+            held[way, step - 1, piece] = (
+                held[way, step - 1, piece].astype(jnp.float32) + parts[goal, piece].astype(jnp.float32)
             ).astype(jnp.bfloat16)
-            src = held.at[way, step - 1, here]
+            src = held.at[way, step - 1, piece]
         else:
-            src = parts.at[goal, here]
-        rs[way, step, piece] = launch(copy_to(src, held.at[way, step, here], rs_s.at[way, step, piece], rs_r.at[way, step, piece], seq=peers[way]))
+            src = parts.at[goal, piece]
+        rs[way, step, piece] = launch(copy_to(src, held.at[way, step, piece], rs_s.at[way, step, piece], rs_r.at[way, step, piece], seq=peers[way]))
 
     part(at(steps))
     rs_send(0, 0, 0)
@@ -459,14 +510,22 @@
         for piece in (0, 1):
             for way in (0, 1):
                 rs_send(way, step, 1 ^ piece ^ way)
-    for piece in (0, 1):
+    late_send(near, 0)
+    for c in (0, 1):
         for way in (0, 1):
-            rs[way, steps - 1, piece].wait_recv()
-    summed = (tok_ref[...].astype(jnp.float32) + parts[me].astype(jnp.float32)
-        + held[0, steps - 1].astype(jnp.float32) + held[1, steps - 1].astype(jnp.float32)).astype(jnp.bfloat16)
-    hidden = summed.astype(jnp.float32)
+            rs[way, steps - 1, c].wait_recv()
+        rows = slice(c * hrows, (c + 1) * hrows)
+        value = (parts[me, c].astype(jnp.float32) + held[0, steps - 1, c].astype(jnp.float32)
+            + held[1, steps - 1, c].astype(jnp.float32))
+        for i in range(0, full, 128):
+            term = value[i // 128 * hrows : (i // 128 + 1) * hrows]
+            hid[rows, i : i + 128] = (hid[rows, i : i + 128] + term).astype(jnp.bfloat16).astype(jnp.float32)
+        term = jnp.concatenate(
+            [value[base : base + trows, k * tail : (k + 1) * tail] for k in range(folds)], axis=0)
+        hid[rows, full:] = (hid[rows, full:] + term).astype(jnp.bfloat16).astype(jnp.float32)
+    hidden = hid[...]
     scale = lax.rsqrt(jnp.sum(hidden * hidden, axis=1, keepdims=True) / width + eps)
-    normed = hidden * scale * attn_gain_ref[...]
+    normed = hidden * scale * attn_gain_ref[...].reshape(1, width)
     shard = wq.shape[1]
     for i in range(count):
         both[core, i] = normed[:, i * shard : (i + 1) * shard].astype(jnp.bfloat16)
@@ -474,20 +533,28 @@
 
     for key in qx:
         qx[key].wait_recv()
-    pair.wait_recv()
-
-    def project(columns):
+
+    def project(m, columns):
         total = None
         for i in range(count):
-            x = both[:, i].reshape(2 * tok_count, shard)
+            x = both[:, i].reshape(2 * tok_count, shard) if m is None else both[m, i]
             term = dot(x, wq[i, :, columns])
             total = term if total is None else total + term
-        return total.astype(jnp.bfloat16).reshape(2, tok_count, -1)
-
-    kv[...] = project(pl.ds(0, 2 * kw))
-    along = launch(copy_to(kv, halo, halo_s.at[0], halo_r.at[0], seq=following))
-    queries[...] = project(pl.ds(2 * kw, qw))
-    along.wait_recv()
+        return total.astype(jnp.bfloat16)
+
+    kv[core] = project(core, pl.ds(0, 2 * kw))
+    along = [launch(copy_to(kv.at[core], halo.at[core], halo_s.at[0], halo_r.at[0], seq=following))]
+    pair.wait_recv()
+    kv[other_core] = project(other_core, pl.ds(0, 2 * kw))
+    along.append(launch(copy_to(kv.at[other_core], halo.at[other_core], halo_s.at[1], halo_r.at[1], seq=following)))
+    late_send(near, 1)
+    queries[...] = project(None, pl.ds(2 * kw, qw)).reshape(2, tok_count, qw)
+    for i in range(0, width, 128):
+        size = min(128, width - i)
+        hid_t[i : i + size, :] = hid[:, i : i + size].T
+    late_send(near + 1, 0)
+    for copy in along:
+        copy.wait_recv()
 
     lane = lax.broadcasted_iota(jnp.int32, (tok_count, 2 * tok_count), 1)
     row = lax.broadcasted_iota(jnp.int32, (tok_count, 2 * tok_count), 0)
@@ -513,12 +580,14 @@
             k_past = stacked(halo[source, :, :kw], head)
             v_past = stacked(halo[source, :, kw:], head)
             for t in range(head * per_head, (head + 1) * per_head):
+                first_head = core * 2 * tiles + 2 * t
+                sink = jnp.exp(jnp.where(left[:1], sink_ref[first_head], sink_ref[first_head + 1]))
                 x = queries[m, :, t * 128 : (t + 1) * 128]
                 score = jnp.where(past, dot(x, k_past, ((1,), (1,))), dot(x, k_own, ((1,), (1,))))
                 weight = jnp.exp(score * (float(HEAD_SIZE) ** -0.5))
                 weight = jnp.where(past & jnp.logical_not(known), 0.0, weight)
                 mass = jnp.where(left, jnp.sum(weight[:, :tok_count], axis=1, keepdims=True),
-                    jnp.sum(weight[:, tok_count:], axis=1, keepdims=True)) + sink_ref[t : t + 1, :]
+                    jnp.sum(weight[:, tok_count:], axis=1, keepdims=True)) + sink
                 probs = weight / mass
                 mixed[m, :, t * 128 : (t + 1) * 128] = (
                     dot(jnp.where(past, 0.0, probs).astype(jnp.bfloat16), v_own)
@@ -526,19 +595,29 @@
                 ).astype(jnp.bfloat16)
 
     for way in (0, 1):
-        for step in range(steps):
+        for step in range(near - 1):
             cond, _, crossing = o_landed(way, step)
 
             @pl.when(cond)
             def _():
                 crossing.wait_recv()
+        cond, landed = late_landed(way, near, 1)
+
+        @pl.when(cond)
+        def _():
+            landed.wait_recv()
+        cond, landed = late_landed(way, near + 1, 0)
+
+        @pl.when(cond)
+        def _():
+            landed.wait_recv()
 
     share = wo.shape[2]
 
     def output(m):
         total = None
         for i in range(steps):
-            term = dot(mixed[m, :, i * share : (i + 1) * share], wo[i], ((1,), (1,)))
+            term = dot(wo[i], mixed[m, :, i * share : (i + 1) * share], ((1,), (1,)))
             total = term if total is None else total + term
         return total
 
@@ -546,7 +625,7 @@
     last = launch(copy_to(given, back, pair_s.at[1], pair_r.at[1], pipe=other_core))
     kept = output(core)
     last.wait_recv()
-    out_ref[...] = (hidden + kept + back[...].astype(jnp.float32)).astype(jnp.bfloat16)
+    out_ref[...] = (hid_t[...] + kept + back[...].astype(jnp.float32)).astype(jnp.bfloat16)
     for _, copy in sends:
         copy.wait_send()
     for cond, copy in o_sends:
@@ -560,7 +639,6 @@
     head_sink_logits, out_proj,
 ):
     count = lax.axis_size("seq")
-    core = lax.axis_index("pipe")
     steps = count // 2
     tok_count, width = tokens.shape[1:]
     own = gate_up.shape[0] // 2
@@ -568,18 +646,15 @@
     heads = QUERY_HEADS // 2
     qw = heads * HEAD_SIZE
     kw = KEY_VALUE_HEADS * HEAD_SIZE // 2
-    tok = tokens[0]
-    gain = jnp.pad(moe_gain, (0, -width % 128)).reshape(-1, 128).T
-    sinks = jnp.exp(lax.dynamic_slice_in_dim(head_sink_logits, core * heads, heads))
-    sinks = jnp.repeat(sinks.reshape(heads // 2, 2), tok_count, axis=1)
+    chunk = tok_count // 2 * width // 128
     dma = pltpu.SemaphoreType.DMA
     bf16 = jnp.bfloat16
     vm = pl.BlockSpec(memory_space=pltpu.VMEM)
     hbm = pl.BlockSpec(memory_space=pl.ANY)
     out = pl.pallas_call(
         layer_kernel,
-        out_shape=jax.ShapeDtypeStruct((tok_count, width), bf16),
-        in_specs=[vm] * 7 + [hbm] * 4,
+        out_shape=jax.ShapeDtypeStruct((width, tok_count), bf16),
+        in_specs=[vm] * 5 + [pl.BlockSpec(memory_space=pltpu.SMEM)] + [hbm] * 4,
         out_specs=vm,
         scratch_shapes=[
             pltpu.VMEM((count, width + E, tok_count), bf16),
@@ -590,8 +665,8 @@
             pltpu.VMEM((count * CAP, 2 * half), jnp.float32),
             pltpu.VMEM((2, count * CAP, half), bf16),
             pltpu.VMEM((count, own * CAP, width), bf16),
-            pltpu.VMEM((count, tok_count, width), bf16),
-            pltpu.VMEM((2, steps, tok_count, width), bf16),
+            pltpu.VMEM((count, 2, chunk, 128), bf16),
+            pltpu.VMEM((2, steps, 2, chunk, 128), bf16),
             pltpu.VMEM((count, qkv_proj.shape[0], 2 * kw + qw), bf16),
             pltpu.VMEM((steps, width, out_proj.shape[0]), bf16),
             pltpu.VMEM((2, count, tok_count, qkv_proj.shape[0]), bf16),
@@ -599,19 +674,21 @@
             pltpu.VMEM((2, tok_count, 2 * kw), bf16),
             pltpu.VMEM((2, tok_count, qw), bf16),
             pltpu.VMEM((2, tok_count, qw), bf16),
-            pltpu.VMEM((tok_count, width), bf16),
-            pltpu.VMEM((tok_count, width), bf16),
+            pltpu.VMEM((width, tok_count), bf16),
+            pltpu.VMEM((width, tok_count), bf16),
+            pltpu.VMEM((tok_count, width), jnp.float32),
+            pltpu.VMEM((width, tok_count), jnp.float32),
             dma((2 * own,)), dma((2 * own,)), dma((3,)), dma((1,)),
             dma((2, steps, 2)), dma((2, steps, 2)), dma((2, steps, 2)), dma((2, steps, 2)),
             dma((2, steps)), dma((2, steps)), dma((2, steps)), dma((2, steps)),
             dma((2, steps)), dma((2, steps)), dma((2, steps)), dma((2, steps)),
-            dma((2,)), dma((2,)), dma((1,)), dma((1,)),
+            dma((2, 3)), dma((2, 3)), dma((2,)), dma((2,)), dma((2,)), dma((2,)),
         ],
         compiler_params=pltpu.CompilerParams(
             collective_id=0, has_side_effects=True, vmem_limit_bytes=67043328),
-    )(tok.T, tok, routes[0].T, route_weights[0].T, gain, attn_gain[None], sinks,
+    )(tokens[0].T, routes[0].T, route_weights[0].T, moe_gain, attn_gain, head_sink_logits,
       gate_up, down_proj, qkv_proj, out_proj.T)
-    return out[None]
+    return out.T[None]
 
 
 def solution(mesh):

time: 136 us -> 122 us (0.90)
  Pallas kernels: 128 us -> 120 us
  local copies, waits for them, and re-layouts: 8.11 us -> 1.75 us
    pallas_call x1, Pallas kernels: 128 us -> 120 us  [whole_layer(): pl.pallas_call(layer_kernel, out_shape=jax.ShapeDtypeStruct((width, tok_c...]
    broadcast_in_dim x2 -> x0, local copies, waits for them, and re-layouts: 3.22 us -> none  [the longest x1 1.91 us: whole_layer(): return out[None]]
    reshape x5 -> x0, local copies, waits for them, and re-layouts: 2.26 us -> none  [the longest x2 1.44 us: whole_layer(): gain = jnp.pad(moe_gain, (0, -width % 128)).reshape(-1, 128).T]
where the time goes in v2:
time: 122 us; the launch traced here: 121 us
  Pallas kernels  120 us (98%)
  local copies, waits for them, and re-layouts  1.75 us (1%)
    pallas_call x1, Pallas kernels, whole_layer(): pl.pallas_call(layer_kernel, out_shape=jax.ShapeDtypeStruct((width, tok_c...  120 us

profile of v2, /device:TPU:0, one launch (start us, length us, event | category | flops | bytes accessed | tf_op | source)
XLA Modules:
  0.0 121.4 jit_solution(878557775817127980)
XLA Ops:
  0.0 119.6 %shard_map.100 = bf16[1440,128]{1,0:T(8,128)(2,1)} custom-call(bf16[1440,128]{1,0:T(8,128)(2,1)} %bitcast.15, s32[4,128]{1,0:T(4,128)} %bitcast.16, f32[4,128]{1,0:T(4,128)} %bitcast.17, f32[1440]{0:T(1024)} %gain_ref.1, f32[1440]{0:T(1024)} %attn_gain_ref.1, f32[32]{0:T(128)} %sink_ref.1, bf16[4,1440,1440]{2,1,0:T(8,128)(2,1)} %gate_up_ref.1, ...), custom_call_target="tpu_custom_call" | custom-call | tf_op jit(solution)/shard_map/pallas_call | solution.py:654
  119.6 1.7 %copy.12 = bf16[1,128,1440]{1,2,0:T(8,128)(2,1)} copy(bf16[1,128,1440]{1,2,0:T(8,128)(2,1)} %bitcast.13) | data formatting | bytes 737280

commit v3 on v2

--- a/solution.py
+++ b/solution.py
@@ -196,9 +196,10 @@
     gate_up_ref, down_ref, qkv_ref, out_t_ref,
     out_ref,
     blocks, picked, combine, gu, dn, proj, act, done, parts, held, wq, wo,
-    both, kv, halo, queries, mixed, given, back, hid, hid_t,
+    both, kv, halo, queries, mixed, given, back, hid, hid_t, wkv, kv_other,
     gu_sem, dn_sem, wq_sem, wo_sem, ag_s, ag_r, rs_s, rs_r, q_s, q_r, qx_s, qx_r,
-    o_s, o_r, ox_s, ox_r, late_s, late_r, pair_s, pair_r, halo_s, halo_r,
+    o_s, o_r, ox_s, ox_r, late_s, late_r, lx_s, lx_r, pair_s, pair_r, halo_s, halo_r,
+    wkv_s, wkv_r,
 ):
     count = lax.axis_size("seq")
     steps = count // 2
@@ -220,6 +221,12 @@
         sends.append((None, copy))
         return copy
 
+    barrier = pltpu.get_barrier_semaphore()
+    for device in ({"seq": peers[0]}, {"seq": peers[1]}, {"seq": following}, {"seq": preceding},
+                   {"pipe": other_core}, {"groups": other_group},
+                   {"seq": following, "pipe": other_core}, {"seq": preceding, "pipe": other_core}):
+        pl.semaphore_signal(barrier, inc=1, device_id=device, device_id_type=MESH)
+
     qw, kw = queries.shape[2], kv.shape[2] // 2
     all_q = QUERY_HEADS * HEAD_SIZE
     all_k = KEY_VALUE_HEADS * HEAD_SIZE
@@ -244,26 +251,6 @@
     for copy in gu_copies + dn_copies:
         copy.start()
 
-    tall = tok_t_ref[...].astype(jnp.float32)
-    scale = lax.rsqrt(jnp.sum(tall * tall, axis=0, keepdims=True) / width + eps)
-    for i in range(0, width, 128):
-        size = min(128, width - i)
-        gain = jnp.broadcast_to(gain_ref[pl.ds(i, size)].reshape(1, size), (tok_count, size)).T
-        blocks[me, i : i + size, :] = (
-            tok_t_ref[i : i + size, :].astype(jnp.float32) * scale * gain
-        ).astype(jnp.bfloat16)
-    expert_row = lax.broadcasted_iota(jnp.int32, (E, tok_count), 0)
-    dense = jnp.zeros((E, tok_count), jnp.float32)
-    for j in range(TOP):
-        dense = dense + jnp.where(expert_row == routes_ref[j : j + 1, :], weights_ref[j : j + 1, :], 0.0)
-    blocks[me, width : width + E, :] = dense.astype(jnp.bfloat16)
-
-    barrier = pltpu.get_barrier_semaphore()
-    for device in ({"seq": peers[0]}, {"seq": peers[1]}, {"seq": following}, {"seq": preceding},
-                   {"pipe": other_core}, {"groups": other_group}):
-        pl.semaphore_signal(barrier, inc=1, device_id=device, device_id_type=MESH)
-    pl.semaphore_wait(barrier, 6)
-
     rows_all = blocks.shape[1]
     cut = (rows_all // 2 + 15) // 16 * 16
     pieces = (pl.ds(0, cut), pl.ds(cut, rows_all - cut))
@@ -358,40 +345,47 @@
                     copy.start()
                 o_sends.append((onward, copy))
 
-    def late_copy(way, step, piece):
-        origin = at(-step if way == 0 else step)
-        ref = wo.at[lax.rem(origin, steps), pl.ds(piece * orows, orows)]
-        index = 2 * (step - near) + (piece ^ way)
+    quarter = (orows // 2 + 15) // 16 * 16
+    mid = (orows - quarter // 2 + 15) // 16 * 16
+    crossed = pl.ds(pl.multiple_of(group * (2 * orows - quarter), 16), quarter)
+    inner = (pl.ds(quarter, mid - quarter), pl.ds(mid, 2 * orows - quarter - mid))
+
+    def late_piece(name):
+        return {"x": crossed, "a": inner[0], "b": inner[1]}[name]
+
+    def late_copy(way, step, name, landed=False):
+        hops = step + 1 if landed else step
+        origin = at(-hops if way == 0 else hops)
+        ref = wo.at[lax.rem(origin, steps), late_piece(name)]
+        index = 3 * (step - near) + "xab".index(name)
         return holds(origin), copy_to(ref, ref, late_s.at[way, index], late_r.at[way, index], seq=peers[way])
 
-    def late_send(step, order):
-        for way in (0, 1):
-            cond, copy = late_copy(way, step, order ^ way)
-            if order == 0:
-                if step == near:
-                    _, _, before_it = o_landed(way, step - 1)
-                    before_it_wait = before_it.wait_recv
-                else:
-                    origin_cond, before_it = late_landed(way, step - 1, 0)
-                    before_it_wait = before_it.wait_recv
-
-                @pl.when(cond)
-                def _():
-                    before_it_wait()
-                    copy.start()
-            else:
-                @pl.when(cond)
-                def _():
-                    copy.start()
-            o_sends.append((cond, copy))
-
-    def late_landed(way, step, order):
+    def late_send(way, step, names, after=()):
+        cond, _ = late_copy(way, step, names[0])
+        copies = [late_copy(way, step, name)[1] for name in names]
+
+        @pl.when(cond)
+        def _():
+            for copy in after:
+                copy.wait_recv()
+            for copy in copies:
+                copy.start()
+        o_sends.extend((cond, copy) for copy in copies)
+
+    def late_cross(way, step, index):
+        cond, landed = late_copy(way, step, "x", True)
         origin = at(-step - 1 if way == 0 else step + 1)
-        piece = order ^ way
-        ref = wo.at[lax.rem(origin, steps), pl.ds(piece * orows, orows)]
-        index = 2 * (step - near) + order
-        return holds(origin), copy_to(ref, ref, late_s.at[way, index], late_r.at[way, index], seq=peers[way])
-
+        ref = wo.at[lax.rem(origin, steps), crossed]
+        crossing = copy_to(ref, ref, lx_s.at[index], lx_r.at[index], groups=other_group)
+
+        @pl.when(cond)
+        def _():
+            landed.wait_recv()
+            crossing.start()
+        o_sends.append((cond, crossing))
+        return cond, crossing
+
+    expert_row = lax.broadcasted_iota(jnp.int32, (E, tok_count), 0)
     lane_tok = lax.broadcasted_iota(jnp.int32, (tok_count, tok_count), 1)
     row_tok = lax.broadcasted_iota(jnp.int32, (tok_count, tok_count), 0)
     before = jnp.where(row_tok < lane_tok, 1.0, 0.0).astype(jnp.bfloat16)
@@ -415,10 +409,23 @@
         for e in range(own):
             picked[e, n] = rows[e * CAP : (e + 1) * CAP]
 
+    tall = tok_t_ref[...].astype(jnp.float32)
+    scale = lax.rsqrt(jnp.sum(tall * tall, axis=0, keepdims=True) / width + eps)
+    pl.semaphore_wait(barrier, 8)
+    o_begin()
+    for i in range(0, width, 128):
+        size = min(128, width - i)
+        gain = jnp.broadcast_to(gain_ref[pl.ds(i, size)].reshape(1, size), (tok_count, size)).T
+        blocks[me, i : i + size, :] = (
+            tok_t_ref[i : i + size, :].astype(jnp.float32) * scale * gain
+        ).astype(jnp.bfloat16)
+    dense = jnp.zeros((E, tok_count), jnp.float32)
+    for j in range(TOP):
+        dense = dense + jnp.where(expert_row == routes_ref[j : j + 1, :], weights_ref[j : j + 1, :], 0.0)
+    blocks[me, width : width + E, :] = dense.astype(jnp.bfloat16)
     for piece in (0, 1):
         for way in (0, 1):
             ag_send(way, 0, piece ^ way)
-    o_begin()
     process(me)
     for i in range(0, width, 128):
         size = min(128, width - i)
@@ -504,13 +511,22 @@
         part(at(offset))
         part(at(-offset))
     part(me)
+    for key in qx:
+        if key[1] < steps - 2:
+            qx[key].wait_recv()
     rs_send(0, 1, 0)
     rs_send(1, 1, 1)
     for step in range(2, steps):
         for piece in (0, 1):
             for way in (0, 1):
                 rs_send(way, step, 1 ^ piece ^ way)
-    late_send(near, 0)
+    for key in qx:
+        if key[1] >= steps - 2:
+            qx[key].wait_recv()
+    own_kv = wq.at[:, :, pl.ds(0, 2 * kw)]
+    keys_over = launch(copy_to(own_kv, wkv, wkv_s.at[0], wkv_r.at[0], pipe=other_core))
+    for way in (0, 1):
+        late_send(way, near, "xa" if way == 0 else "bx", (o_landed(way, near - 1)[2],))
     for c in (0, 1):
         for way in (0, 1):
             rs[way, steps - 1, c].wait_recv()
@@ -531,28 +547,34 @@
         both[core, i] = normed[:, i * shard : (i + 1) * shard].astype(jnp.bfloat16)
     pair = launch(copy_to(both.at[core], both.at[core], pair_s.at[0], pair_r.at[0], pipe=other_core))
 
-    for key in qx:
-        qx[key].wait_recv()
-
-    def project(m, columns):
+    def project(m, weights, columns):
         total = None
         for i in range(count):
             x = both[:, i].reshape(2 * tok_count, shard) if m is None else both[m, i]
-            term = dot(x, wq[i, :, columns])
+            term = dot(x, weights[i, :, columns])
             total = term if total is None else total + term
         return total.astype(jnp.bfloat16)
 
-    kv[core] = project(core, pl.ds(0, 2 * kw))
+    pairs_cols = pl.ds(0, 2 * kw)
+    kv[core] = project(core, wq, pairs_cols)
     along = [launch(copy_to(kv.at[core], halo.at[core], halo_s.at[0], halo_r.at[0], seq=following))]
+    keys_over.wait_recv()
+    kv_other[...] = project(core, wkv, pairs_cols)
+    along.append(launch(copy_to(kv_other, halo.at[core], halo_s.at[1], halo_r.at[1], seq=following, pipe=other_core)))
+    beside = launch(copy_to(kv_other, kv.at[core], pair_s.at[2], pair_r.at[2], pipe=other_core))
+    for way in (0, 1):
+        late_send(way, near, "b" if way == 0 else "a")
+    crossings = [late_cross(0, near, 0)]
     pair.wait_recv()
-    kv[other_core] = project(other_core, pl.ds(0, 2 * kw))
-    along.append(launch(copy_to(kv.at[other_core], halo.at[other_core], halo_s.at[1], halo_r.at[1], seq=following)))
-    late_send(near, 1)
-    queries[...] = project(None, pl.ds(2 * kw, qw)).reshape(2, tok_count, qw)
+    queries[...] = project(None, wq, pl.ds(2 * kw, qw)).reshape(2, tok_count, qw)
+    late_send(0, near + 1, "xa", (late_copy(0, near, "a", True)[1],))
+    late_send(1, near + 1, "b", (late_copy(1, near, "b", True)[1],))
+    crossings.append(late_cross(1, near, 1))
     for i in range(0, width, 128):
         size = min(128, width - i)
         hid_t[i : i + size, :] = hid[:, i : i + size].T
-    late_send(near + 1, 0)
+    crossings.append(late_cross(0, near + 1, 2))
+    beside.wait_recv()
     for copy in along:
         copy.wait_recv()
 
@@ -586,9 +608,9 @@
                 score = jnp.where(past, dot(x, k_past, ((1,), (1,))), dot(x, k_own, ((1,), (1,))))
                 weight = jnp.exp(score * (float(HEAD_SIZE) ** -0.5))
                 weight = jnp.where(past & jnp.logical_not(known), 0.0, weight)
-                mass = jnp.where(left, jnp.sum(weight[:, :tok_count], axis=1, keepdims=True),
-                    jnp.sum(weight[:, tok_count:], axis=1, keepdims=True)) + sink
-                probs = weight / mass
+                mass_a = jnp.sum(weight[:, :tok_count], axis=1, keepdims=True) + sink[:, :1]
+                mass_b = jnp.sum(weight[:, tok_count:], axis=1, keepdims=True) + sink[:, tok_count : tok_count + 1]
+                probs = weight * jnp.where(left, 1.0 / mass_a, 1.0 / mass_b)
                 mixed[m, :, t * 128 : (t + 1) * 128] = (
                     dot(jnp.where(past, 0.0, probs).astype(jnp.bfloat16), v_own)
                     + dot(jnp.where(past, probs, 0.0).astype(jnp.bfloat16), v_past)
@@ -601,16 +623,22 @@
             @pl.when(cond)
             def _():
                 crossing.wait_recv()
-        cond, landed = late_landed(way, near, 1)
+        cond, landed = late_copy(way, near, "b" if way == 0 else "a", True)
 
         @pl.when(cond)
         def _():
             landed.wait_recv()
-        cond, landed = late_landed(way, near + 1, 0)
-
+    cond, landed = late_copy(0, near + 1, "a", True)
+    _, landed_b = late_copy(1, near + 1, "b", True)
+
+    @pl.when(cond)
+    def _():
+        landed.wait_recv()
+        landed_b.wait_recv()
+    for cond, crossing in crossings:
         @pl.when(cond)
         def _():
-            landed.wait_recv()
+            crossing.wait_recv()
 
     share = wo.shape[2]
 
@@ -678,11 +706,14 @@
             pltpu.VMEM((width, tok_count), bf16),
             pltpu.VMEM((tok_count, width), jnp.float32),
             pltpu.VMEM((width, tok_count), jnp.float32),
+            pltpu.VMEM((count, qkv_proj.shape[0], 2 * kw), bf16),
+            pltpu.VMEM((tok_count, 2 * kw), bf16),
             dma((2 * own,)), dma((2 * own,)), dma((3,)), dma((1,)),
             dma((2, steps, 2)), dma((2, steps, 2)), dma((2, steps, 2)), dma((2, steps, 2)),
             dma((2, steps)), dma((2, steps)), dma((2, steps)), dma((2, steps)),
             dma((2, steps)), dma((2, steps)), dma((2, steps)), dma((2, steps)),
-            dma((2, 3)), dma((2, 3)), dma((2,)), dma((2,)), dma((2,)), dma((2,)),
+            dma((2, 6)), dma((2, 6)), dma((3,)), dma((3,)), dma((3,)), dma((3,)), dma((2,)), dma((2,)),
+            dma((1,)), dma((1,)),
         ],
         compiler_params=pltpu.CompilerParams(
             collective_id=0, has_side_effects=True, vmem_limit_bytes=67043328),

time: 122 us -> 126 us (1.033)
  Pallas kernels: 120 us -> 124 us
    pallas_call x1, Pallas kernels: 120 us -> 124 us  [whole_layer(): pl.pallas_call(layer_kernel, out_shape=jax.ShapeDtypeStruct((width, tok_c...]
where the time goes in v3:
time: 126 us
  Pallas kernels  124 us (98%)
  local copies, waits for them, and re-layouts  1.75 us (1%)
    pallas_call x1, Pallas kernels, whole_layer(): pl.pallas_call(layer_kernel, out_shape=jax.ShapeDtypeStruct((width, tok_c...  124 us

profile of v3, /device:TPU:0, one launch (start us, length us, event | category | flops | bytes accessed | tf_op | source)
XLA Modules:
  0.0 125.6 jit_solution(17508752432003506038)
XLA Ops:
  0.0 123.8 %shard_map.100 = bf16[1440,128]{1,0:T(8,128)(2,1)} custom-call(bf16[1440,128]{1,0:T(8,128)(2,1)} %bitcast.15, s32[4,128]{1,0:T(4,128)} %bitcast.16, f32[4,128]{1,0:T(4,128)} %bitcast.17, f32[1440]{0:T(1024)} %gain_ref.1, f32[1440]{0:T(1024)} %attn_gain_ref.1, f32[32]{0:T(128)} %sink_ref.1, bf16[4,1440,1440]{2,1,0:T(8,128)(2,1)} %gate_up_ref.1, ...), custom_call_target="tpu_custom_call" | custom-call | tf_op jit(solution)/shard_map/pallas_call | solution.py:682
  123.9 1.7 %copy.12 = bf16[1,128,1440]{1,2,0:T(8,128)(2,1)} copy(bf16[1,128,1440]{1,2,0:T(8,128)(2,1)} %bitcast.13) | data formatting | bytes 737280

commit v4 on v2

--- a/solution.py
+++ b/solution.py
@@ -198,7 +198,7 @@
     blocks, picked, combine, gu, dn, proj, act, done, parts, held, wq, wo,
     both, kv, halo, queries, mixed, given, back, hid, hid_t,
     gu_sem, dn_sem, wq_sem, wo_sem, ag_s, ag_r, rs_s, rs_r, q_s, q_r, qx_s, qx_r,
-    o_s, o_r, ox_s, ox_r, late_s, late_r, pair_s, pair_r, halo_s, halo_r,
+    o_s, o_r, ox_s, ox_r, side_s, side_r, feed_s, feed_r, fx_s, fx_r, pair_s, pair_r, halo_s, halo_r,
 ):
     count = lax.axis_size("seq")
     steps = count // 2
@@ -210,7 +210,19 @@
     slots = own * CAP
     place = ring_place(me, count, True)
     at = lambda offset: ring_index(lax.rem(place + offset + count, count), count, True)
+    spot = lambda p: ring_index(lax.rem(p + count, count), count, True)
     peers = (at(1), at(-1))
+    column = lax.rem(place, steps)
+    inner = (column > 0) & (column < steps - 1)
+    corner = jnp.logical_not(inner)
+    low = column < steps // 2
+    toward = jnp.where(low, 1, -1)
+    outward = (jnp.logical_not(low), low)
+    inner_out = [inner & outward[way] for way in (0, 1)]
+    inner_in = [inner & jnp.logical_not(outward[way]) for way in (0, 1)]
+    corner_fresh = [corner & outward[way] for way in (0, 1)]
+    beside_place = count - 1 - place
+    beside = spot(beside_place)
     following, preceding = lax.rem(me + 1, count), lax.rem(me + count - 1, count)
     other_core, other_group = 1 - core, 1 - group
     sends = []
@@ -260,9 +272,9 @@
 
     barrier = pltpu.get_barrier_semaphore()
     for device in ({"seq": peers[0]}, {"seq": peers[1]}, {"seq": following}, {"seq": preceding},
-                   {"pipe": other_core}, {"groups": other_group}):
+                   {"pipe": other_core}, {"groups": other_group}, {"seq": beside}):
         pl.semaphore_signal(barrier, inc=1, device_id=device, device_id_type=MESH)
-    pl.semaphore_wait(barrier, 6)
+    pl.semaphore_wait(barrier, 7)
 
     rows_all = blocks.shape[1]
     cut = (rows_all // 2 + 15) // 16 * 16
@@ -358,39 +370,64 @@
                     copy.start()
                 o_sends.append((onward, copy))
 
-    def late_copy(way, step, piece):
-        origin = at(-step if way == 0 else step)
-        ref = wo.at[lax.rem(origin, steps), pl.ds(piece * orows, orows)]
-        index = 2 * (step - near) + (piece ^ way)
-        return holds(origin), copy_to(ref, ref, late_s.at[way, index], late_r.at[way, index], seq=peers[way])
-
-    def late_send(step, order):
+    def o_crossed(step):
         for way in (0, 1):
-            cond, copy = late_copy(way, step, order ^ way)
-            if order == 0:
-                if step == near:
-                    _, _, before_it = o_landed(way, step - 1)
-                    before_it_wait = before_it.wait_recv
-                else:
-                    origin_cond, before_it = late_landed(way, step - 1, 0)
-                    before_it_wait = before_it.wait_recv
-
-                @pl.when(cond)
-                def _():
-                    before_it_wait()
-                    copy.start()
-            else:
-                @pl.when(cond)
-                def _():
-                    copy.start()
-            o_sends.append((cond, copy))
-
-    def late_landed(way, step, order):
-        origin = at(-step - 1 if way == 0 else step + 1)
-        piece = order ^ way
-        ref = wo.at[lax.rem(origin, steps), pl.ds(piece * orows, orows)]
-        index = 2 * (step - near) + order
-        return holds(origin), copy_to(ref, ref, late_s.at[way, index], late_r.at[way, index], seq=peers[way])
+            cond, _, crossing = o_landed(way, step)
+
+            @pl.when(cond)
+            def _():
+                crossing.wait_recv()
+
+    def side_copy(origin, hop):
+        ref = wo.at[lax.rem(origin, steps)]
+        return inner & holds(origin), copy_to(ref, ref, side_s.at[hop], side_r.at[hop], seq=beside)
+
+    def side_send(hop):
+        cond, copy = side_copy(at(toward * hop), hop)
+
+        @pl.when(cond)
+        def _():
+            copy.start()
+        o_sends.append((cond, copy))
+
+    def side_wait(hop):
+        cond, copy = side_copy(spot(beside_place - toward * hop), hop)
+
+        @pl.when(cond)
+        def _():
+            copy.wait_recv()
+
+    feed_part = pl.ds(pl.multiple_of(group * orows, 16), orows)
+
+    def feed_copy(origin, index):
+        ref = wo.at[lax.rem(origin, steps), feed_part]
+        return holds(origin), copy_to(ref, ref, feed_s.at[index], feed_r.at[index], seq=spot(place - toward))
+
+    def feed_send():
+        for index, origin in enumerate((
+            at(2 * toward), spot(beside_place - toward), spot(beside_place - 2 * toward))):
+            cond, copy = feed_copy(origin, index)
+
+            @pl.when(inner & cond)
+            def _():
+                copy.start()
+            o_sends.append((inner & cond, copy))
+
+    feed_crossings = []
+
+    def feed_cross(index):
+        origin = (spot(place + 3 * toward), spot(beside_place - 2 * toward), spot(beside_place - 3 * toward))[index]
+        held_here, landed = feed_copy(origin, index)
+        cond = corner & held_here
+        ref = wo.at[lax.rem(origin, steps), feed_part]
+        crossing = copy_to(ref, ref, fx_s.at[index], fx_r.at[index], groups=other_group)
+
+        @pl.when(cond)
+        def _():
+            landed.wait_recv()
+            crossing.start()
+        o_sends.append((cond, crossing))
+        feed_crossings.append((cond, crossing))
 
     lane_tok = lax.broadcasted_iota(jnp.int32, (tok_count, tok_count), 1)
     row_tok = lax.broadcasted_iota(jnp.int32, (tok_count, tok_count), 0)
@@ -419,6 +456,7 @@
         for way in (0, 1):
             ag_send(way, 0, piece ^ way)
     o_begin()
+    side_send(0)
     process(me)
     for i in range(0, width, 128):
         size = min(128, width - i)
@@ -431,12 +469,17 @@
                     ag_send(way, step, piece ^ way)
         if step <= near:
             o_step(step)
+        else:
+            o_crossed(step - near - 1)
+            side_send(1)
         process(at(-step))
         process(at(step))
     ag[0, steps - 1, 0].wait_recv()
     ag[1, steps - 1, 1].wait_recv()
     process(at(steps))
 
+    o_crossed(1)
+    side_send(2)
     q_begin()
     pos = {0: 1, 1: 2, 2: 3, 3: 4}
     half = dn.shape[1]
@@ -482,17 +525,33 @@
 
     rs = {}
 
+    def rs_add(goal, way, step, piece):
+        here = held.at[way, step, piece]
+        copy_to(here, here, rs_s.at[0, step, piece], rs_r.at[way, step, piece], seq=peers[0]).wait_recv()
+        parts[goal, piece] = (
+            parts[goal, piece].astype(jnp.float32) + held[way, step, piece].astype(jnp.float32)
+        ).astype(jnp.bfloat16)
+
     def rs_send(way, step, piece):
         goal = at((steps - step) * (1 if way == 0 else -1))
         if (way, step - 1, piece) in rs:
-            rs[way, step - 1, piece].wait_recv()
-            held[way, step - 1, piece] = (
-                held[way, step - 1, piece].astype(jnp.float32) + parts[goal, piece].astype(jnp.float32)
-            ).astype(jnp.bfloat16)
-            src = held.at[way, step - 1, piece]
-        else:
-            src = parts.at[goal, piece]
-        rs[way, step, piece] = launch(copy_to(src, held.at[way, step, piece], rs_s.at[way, step, piece], rs_r.at[way, step, piece], seq=peers[way]))
+            @pl.when(jnp.logical_not(corner_fresh[way]))
+            def _():
+                rs_add(goal, way, step - 1, piece)
+        if step == steps - 1:
+            @pl.when(inner_out[way])
+            def _():
+                rs_add(goal, 2, 2, piece)
+            if piece == way:
+                @pl.when(inner_in[way])
+                def _():
+                    rs_add(goal, 2, 0, piece)
+        landing, peer = way, peers[way]
+        if step < steps - 1:
+            landing = jnp.where(inner_out[way], 2, way)
+            peer = jnp.where(inner_out[way], beside, peer)
+        rs[way, step, piece] = launch(copy_to(parts.at[goal, piece], held.at[landing, step, piece],
+            rs_s.at[way, step, piece], rs_r.at[landing, step, piece], seq=peer))
 
     part(at(steps))
     rs_send(0, 0, 0)
@@ -504,16 +563,24 @@
         part(at(offset))
         part(at(-offset))
     part(me)
+    for hop in range(3):
+        side_wait(hop)
+    feed_send()
     rs_send(0, 1, 0)
     rs_send(1, 1, 1)
     for step in range(2, steps):
         for piece in (0, 1):
             for way in (0, 1):
                 rs_send(way, step, 1 ^ piece ^ way)
-    late_send(near, 0)
+        feed_cross(step - 2)
+    feed_cross(2)
     for c in (0, 1):
+        @pl.when(inner)
+        def _():
+            rs_add(me, 2, 1, c)
         for way in (0, 1):
-            rs[way, steps - 1, c].wait_recv()
+            copy_to(held.at[way, steps - 1, c], held.at[way, steps - 1, c], rs_s.at[way, steps - 1, c],
+                rs_r.at[way, steps - 1, c], seq=peers[way]).wait_recv()
         rows = slice(c * hrows, (c + 1) * hrows)
         value = (parts[me, c].astype(jnp.float32) + held[0, steps - 1, c].astype(jnp.float32)
             + held[1, steps - 1, c].astype(jnp.float32))
@@ -547,12 +614,10 @@
     pair.wait_recv()
     kv[other_core] = project(other_core, pl.ds(0, 2 * kw))
     along.append(launch(copy_to(kv.at[other_core], halo.at[other_core], halo_s.at[1], halo_r.at[1], seq=following)))
-    late_send(near, 1)
     queries[...] = project(None, pl.ds(2 * kw, qw)).reshape(2, tok_count, qw)
     for i in range(0, width, 128):
         size = min(128, width - i)
         hid_t[i : i + size, :] = hid[:, i : i + size].T
-    late_send(near + 1, 0)
     for copy in along:
         copy.wait_recv()
 
@@ -594,23 +659,10 @@
                     + dot(jnp.where(past, probs, 0.0).astype(jnp.bfloat16), v_past)
                 ).astype(jnp.bfloat16)
 
-    for way in (0, 1):
-        for step in range(near - 1):
-            cond, _, crossing = o_landed(way, step)
-
-            @pl.when(cond)
-            def _():
-                crossing.wait_recv()
-        cond, landed = late_landed(way, near, 1)
-
+    for cond, crossing in feed_crossings:
         @pl.when(cond)
         def _():
-            landed.wait_recv()
-        cond, landed = late_landed(way, near + 1, 0)
-
-        @pl.when(cond)
-        def _():
-            landed.wait_recv()
+            crossing.wait_recv()
 
     share = wo.shape[2]
 
@@ -666,7 +718,7 @@
             pltpu.VMEM((2, count * CAP, half), bf16),
             pltpu.VMEM((count, own * CAP, width), bf16),
             pltpu.VMEM((count, 2, chunk, 128), bf16),
-            pltpu.VMEM((2, steps, 2, chunk, 128), bf16),
+            pltpu.VMEM((3, steps, 2, chunk, 128), bf16),
             pltpu.VMEM((count, qkv_proj.shape[0], 2 * kw + qw), bf16),
             pltpu.VMEM((steps, width, out_proj.shape[0]), bf16),
             pltpu.VMEM((2, count, tok_count, qkv_proj.shape[0]), bf16),
@@ -679,10 +731,10 @@
             pltpu.VMEM((tok_count, width), jnp.float32),
             pltpu.VMEM((width, tok_count), jnp.float32),
             dma((2 * own,)), dma((2 * own,)), dma((3,)), dma((1,)),
-            dma((2, steps, 2)), dma((2, steps, 2)), dma((2, steps, 2)), dma((2, steps, 2)),
+            dma((2, steps, 2)), dma((2, steps, 2)), dma((2, steps, 2)), dma((3, steps, 2)),
             dma((2, steps)), dma((2, steps)), dma((2, steps)), dma((2, steps)),
             dma((2, steps)), dma((2, steps)), dma((2, steps)), dma((2, steps)),
-            dma((2, 3)), dma((2, 3)), dma((2,)), dma((2,)), dma((2,)), dma((2,)),
+            dma((3,)), dma((3,)), dma((3,)), dma((3,)), dma((3,)), dma((3,)), dma((2,)), dma((2,)), dma((2,)), dma((2,)),
         ],
         compiler_params=pltpu.CompilerParams(
             collective_id=0, has_side_effects=True, vmem_limit_bytes=67043328),
@@ -711,6 +763,7 @@
         and group_count == 2
         and seq_count % 2 == 0
         and 2 * E // seq_count == 4
+        and seq_count == 8
         and QUERY_HEADS % (2 * seq_count) == 0
     )
     return jax.shard_map(

time: 122 us -> 119 us (0.975)
  Pallas kernels: 120 us -> 117 us
    pallas_call x1, Pallas kernels: 120 us -> 117 us  [whole_layer(): pl.pallas_call(layer_kernel, out_shape=jax.ShapeDtypeStruct((width, tok_c...]
where the time goes in v4:
time: 119 us
  Pallas kernels  117 us (98%)
  local copies, waits for them, and re-layouts  1.75 us (1%)
    pallas_call x1, Pallas kernels, whole_layer(): pl.pallas_call(layer_kernel, out_shape=jax.ShapeDtypeStruct((width, tok_c...  117 us

profile of v4, /device:TPU:0, one launch (start us, length us, event | category | flops | bytes accessed | tf_op | source)
XLA Modules:
  0.0 118.8 jit_solution(15057250339390772876)
XLA Ops:
  0.0 117.0 %shard_map.100 = bf16[1440,128]{1,0:T(8,128)(2,1)} custom-call(bf16[1440,128]{1,0:T(8,128)(2,1)} %bitcast.15, s32[4,128]{1,0:T(4,128)} %bitcast.16, f32[4,128]{1,0:T(4,128)} %bitcast.17, f32[1440]{0:T(1024)} %gain_ref.1, f32[1440]{0:T(1024)} %attn_gain_ref.1, f32[32]{0:T(128)} %sink_ref.1, bf16[4,1440,1440]{2,1,0:T(8,128)(2,1)} %gate_up_ref.1, ...), custom_call_target="tpu_custom_call" | custom-call | tf_op jit(solution)/shard_map/pallas_call | solution.py:706
  117.0 1.7 %copy.12 = bf16[1,128,1440]{1,2,0:T(8,128)(2,1)} copy(bf16[1,128,1440]{1,2,0:T(8,128)(2,1)} %bitcast.13) | data formatting | bytes 737280

commit v5 on v4

--- a/solution.py
+++ b/solution.py
@@ -196,7 +196,7 @@
     gate_up_ref, down_ref, qkv_ref, out_t_ref,
     out_ref,
     blocks, picked, combine, gu, dn, proj, act, done, parts, held, wq, wo,
-    both, kv, halo, queries, mixed, given, back, hid, hid_t,
+    both, kv, halo, queries, mixed, given, back, hid, hid_t, passed,
     gu_sem, dn_sem, wq_sem, wo_sem, ag_s, ag_r, rs_s, rs_r, q_s, q_r, qx_s, qx_r,
     o_s, o_r, ox_s, ox_r, side_s, side_r, feed_s, feed_r, fx_s, fx_r, pair_s, pair_r, halo_s, halo_r,
 ):
@@ -232,6 +232,10 @@
         sends.append((None, copy))
         return copy
 
+    barrier = pltpu.get_barrier_semaphore()
+    for device in ({"seq": peers[0]}, {"seq": peers[1]}, {"seq": following}, {"seq": preceding},
+                   {"pipe": other_core}, {"groups": other_group}, {"seq": beside}):
+        pl.semaphore_signal(barrier, inc=1, device_id=device, device_id_type=MESH)
     qw, kw = queries.shape[2], kv.shape[2] // 2
     all_q = QUERY_HEADS * HEAD_SIZE
     all_k = KEY_VALUE_HEADS * HEAD_SIZE
@@ -270,10 +274,6 @@
         dense = dense + jnp.where(expert_row == routes_ref[j : j + 1, :], weights_ref[j : j + 1, :], 0.0)
     blocks[me, width : width + E, :] = dense.astype(jnp.bfloat16)
 
-    barrier = pltpu.get_barrier_semaphore()
-    for device in ({"seq": peers[0]}, {"seq": peers[1]}, {"seq": following}, {"seq": preceding},
-                   {"pipe": other_core}, {"groups": other_group}, {"seq": beside}):
-        pl.semaphore_signal(barrier, inc=1, device_id=device, device_id_type=MESH)
     pl.semaphore_wait(barrier, 7)
 
     rows_all = blocks.shape[1]
@@ -607,19 +607,18 @@
             x = both[:, i].reshape(2 * tok_count, shard) if m is None else both[m, i]
             term = dot(x, wq[i, :, columns])
             total = term if total is None else total + term
-        return total.astype(jnp.bfloat16)
-
-    kv[core] = project(core, pl.ds(0, 2 * kw))
+        return total
+
+    kv[core] = project(core, pl.ds(0, 2 * kw)).astype(jnp.bfloat16)
     along = [launch(copy_to(kv.at[core], halo.at[core], halo_s.at[0], halo_r.at[0], seq=following))]
-    pair.wait_recv()
-    kv[other_core] = project(other_core, pl.ds(0, 2 * kw))
-    along.append(launch(copy_to(kv.at[other_core], halo.at[other_core], halo_s.at[1], halo_r.at[1], seq=following)))
-    queries[...] = project(None, pl.ds(2 * kw, qw)).reshape(2, tok_count, qw)
     for i in range(0, width, 128):
         size = min(128, width - i)
         hid_t[i : i + size, :] = hid[:, i : i + size].T
-    for copy in along:
-        copy.wait_recv()
+    pair.wait_recv()
+    kv[other_core] = project(other_core, pl.ds(0, 2 * kw)).astype(jnp.bfloat16)
+    along.append(launch(copy_to(kv.at[other_core], halo.at[other_core], halo_s.at[1], halo_r.at[1], seq=following)))
+    packed = project(None, pl.ds(2 * kw, qw)).astype(jnp.bfloat16)
+    queries[...] = (packed * (float(HEAD_SIZE) ** -0.5)).reshape(2, tok_count, qw)
 
     lane = lax.broadcasted_iota(jnp.int32, (tok_count, 2 * tok_count), 1)
     row = lax.broadcasted_iota(jnp.int32, (tok_count, 2 * tok_count), 0)
@@ -636,48 +635,77 @@
 
     tiles = qw // 128
     per_head = tiles // 2
-    for m in range(2):
-        source = jnp.where(me == 0, 0, m)
-        known = (me > 0) if m == 0 else (me >= 0)
+
+    def attention(m, known):
+        past_kv = passed[...]
+        dropped = past & jnp.logical_not(known)
         for head in range(2):
             k_own = stacked(kv[m, :, :kw], head)
             v_own = stacked(kv[m, :, kw:], head)
-            k_past = stacked(halo[source, :, :kw], head)
-            v_past = stacked(halo[source, :, kw:], head)
+            k_past = stacked(past_kv[:, :kw], head)
+            v_past = stacked(past_kv[:, kw:], head)
             for t in range(head * per_head, (head + 1) * per_head):
                 first_head = core * 2 * tiles + 2 * t
-                sink = jnp.exp(jnp.where(left[:1], sink_ref[first_head], sink_ref[first_head + 1]))
+                sink_a = jnp.exp(jnp.full((1, 1), sink_ref[first_head]))
+                sink_b = jnp.exp(jnp.full((1, 1), sink_ref[first_head + 1]))
                 x = queries[m, :, t * 128 : (t + 1) * 128]
                 score = jnp.where(past, dot(x, k_past, ((1,), (1,))), dot(x, k_own, ((1,), (1,))))
-                weight = jnp.exp(score * (float(HEAD_SIZE) ** -0.5))
-                weight = jnp.where(past & jnp.logical_not(known), 0.0, weight)
-                mass = jnp.where(left, jnp.sum(weight[:, :tok_count], axis=1, keepdims=True),
-                    jnp.sum(weight[:, tok_count:], axis=1, keepdims=True)) + sink
-                probs = weight / mass
+                weight = jnp.where(dropped, 0.0, jnp.exp(score))
+                mass_a = jnp.sum(weight[:, :tok_count], axis=1, keepdims=True) + sink_a
+                mass_b = jnp.sum(weight[:, tok_count:], axis=1, keepdims=True) + sink_b
+                probs = weight * jnp.where(left, 1.0 / mass_a, 1.0 / mass_b)
                 mixed[m, :, t * 128 : (t + 1) * 128] = (
                     dot(jnp.where(past, 0.0, probs).astype(jnp.bfloat16), v_own)
                     + dot(jnp.where(past, probs, 0.0).astype(jnp.bfloat16), v_past)
                 ).astype(jnp.bfloat16)
 
-    for cond, crossing in feed_crossings:
-        @pl.when(cond)
-        def _():
-            crossing.wait_recv()
-
     share = wo.shape[2]
+    last = copy_to(given, back, pair_s.at[1], pair_r.at[1], pipe=other_core)
 
     def output(m):
         total = None
         for i in range(steps):
             term = dot(wo[i], mixed[m, :, i * share : (i + 1) * share], ((1,), (1,)))
             total = term if total is None else total + term
-        return total
-
-    given[...] = output(other_core).astype(jnp.bfloat16)
-    last = launch(copy_to(given, back, pair_s.at[1], pair_r.at[1], pipe=other_core))
-    kept = output(core)
+
+        @pl.when(m == other_core)
+        def _():
+            given[...] = total.astype(jnp.bfloat16)
+            last.start()
+
+        @pl.when(m == core)
+        def _():
+            hid_t[...] = hid_t[...] + total
+
+    early = jnp.where(me == 0, 0, other_core)
+    late = 1 - early
+
+    @pl.when(me > 0)
+    def _():
+        for copy in along:
+            copy.wait_recv()
+        passed[...] = halo[other_core]
+
+    @pl.when(me == 0)
+    def _():
+        passed[...] = jnp.zeros_like(passed)
+    attention(early, me > 0)
+    for cond, crossing in feed_crossings:
+        @pl.when(cond)
+        def _():
+            crossing.wait_recv()
+    output(early)
+
+    @pl.when(me == 0)
+    def _():
+        for copy in along:
+            copy.wait_recv()
+    passed[...] = halo[jnp.where(me == 0, 0, core)]
+    attention(late, me >= 0)
+    output(late)
     last.wait_recv()
-    out_ref[...] = (hid_t[...] + kept + back[...].astype(jnp.float32)).astype(jnp.bfloat16)
+    out_ref[...] = (hid_t[...] + back[...].astype(jnp.float32)).astype(jnp.bfloat16)
+    last.wait_send()
     for _, copy in sends:
         copy.wait_send()
     for cond, copy in o_sends:
@@ -730,6 +758,7 @@
             pltpu.VMEM((width, tok_count), bf16),
             pltpu.VMEM((tok_count, width), jnp.float32),
             pltpu.VMEM((width, tok_count), jnp.float32),
+            pltpu.VMEM((tok_count, 2 * kw), bf16),
             dma((2 * own,)), dma((2 * own,)), dma((3,)), dma((1,)),
             dma((2, steps, 2)), dma((2, steps, 2)), dma((2, steps, 2)), dma((3, steps, 2)),
             dma((2, steps)), dma((2, steps)), dma((2, steps)), dma((2, steps)),

time: 119 us -> 117 us (0.983)
  Pallas kernels: 117 us -> 114 us
    pallas_call x1, Pallas kernels: 117 us -> 114 us  [whole_layer(): pl.pallas_call(layer_kernel, out_shape=jax.ShapeDtypeStruct((width, tok_c...]
where the time goes in v5:
time: 117 us; the launch traced here: 116 us
  Pallas kernels  114 us (97%)
  local copies, waits for them, and re-layouts  1.75 us (1%)
    pallas_call x1, Pallas kernels, whole_layer(): pl.pallas_call(layer_kernel, out_shape=jax.ShapeDtypeStruct((width, tok_c...  114 us

profile of v5, /device:TPU:0, one launch (start us, length us, event | category | flops | bytes accessed | tf_op | source)
XLA Modules:
  0.0 115.6 jit_solution(10676892703283303126)
XLA Ops:
  0.0 113.9 %shard_map.100 = bf16[1440,128]{1,0:T(8,128)(2,1)} custom-call(bf16[1440,128]{1,0:T(8,128)(2,1)} %bitcast.15, s32[4,128]{1,0:T(4,128)} %bitcast.16, f32[4,128]{1,0:T(4,128)} %bitcast.17, f32[1440]{0:T(1024)} %gain_ref.1, f32[1440]{0:T(1024)} %attn_gain_ref.1, f32[32]{0:T(128)} %sink_ref.1, bf16[4,1440,1440]{2,1,0:T(8,128)(2,1)} %gate_up_ref.1, ...), custom_call_target="tpu_custom_call" | custom-call | tf_op jit(solution)/shard_map/pallas_call | solution.py:734
  113.9 1.7 %copy.12 = bf16[1,128,1440]{1,2,0:T(8,128)(2,1)} copy(bf16[1,128,1440]{1,2,0:T(8,128)(2,1)} %bitcast.13) | data formatting | bytes 737280

commit v6 on v5

--- a/solution.py
+++ b/solution.py
@@ -198,7 +198,7 @@
     blocks, picked, combine, gu, dn, proj, act, done, parts, held, wq, wo,
     both, kv, halo, queries, mixed, given, back, hid, hid_t, passed,
     gu_sem, dn_sem, wq_sem, wo_sem, ag_s, ag_r, rs_s, rs_r, q_s, q_r, qx_s, qx_r,
-    o_s, o_r, ox_s, ox_r, side_s, side_r, feed_s, feed_r, fx_s, fx_r, pair_s, pair_r, halo_s, halo_r,
+    o_s, o_r, ox_s, ox_r, far_s, far_r, far_xs, far_xr, side_s, side_r, feed_s, feed_r, fx_s, fx_r, pair_s, pair_r, halo_s, halo_r,
 ):
     count = lax.axis_size("seq")
     steps = count // 2
@@ -287,36 +287,60 @@
         ag[way, step, piece] = launch(copy_to(ref, ref, ag_s.at[way, step, piece], ag_r.at[way, step, piece], seq=peers[way]))
 
     qcols = wq.shape[2] // 2
-    qcut = (qcols // 2 + 127) // 128 * 128
     q = {}
     qx = {}
 
-    def q_part(way, step):
-        base = pl.multiple_of(group * qcols, 128)
-        if step < steps - 1:
-            return pl.ds(base, qcols)
-        return pl.ds(base, qcut) if way == 0 else pl.ds(base + qcut, qcols - qcut)
+    qpart = pl.ds(pl.multiple_of(group * qcols, 128), qcols)
+    near = steps // 2
 
     def q_send(way, step):
-        ref = wq.at[at(-step if way == 0 else step), :, q_part(way, step)]
+        ref = wq.at[at(-step if way == 0 else step), :, qpart]
         q[way, step] = launch(copy_to(ref, ref, q_s.at[way, step], q_r.at[way, step], seq=peers[way]))
 
     def q_cross(way, step):
         q[way, step].wait_recv()
-        ref = wq.at[at(-step - 1 if way == 0 else step + 1), :, q_part(way, step)]
+        ref = wq.at[at(-step - 1 if way == 0 else step + 1), :, qpart]
         qx[way, step] = launch(copy_to(ref, ref, qx_s.at[way, step], qx_r.at[way, step], groups=other_group))
 
     def q_begin():
-        for copy in wq_copies:
-            copy.wait()
         for way in (0, 1):
             q_send(way, 0)
 
     def q_step(step):
         for way in (0, 1):
             q_cross(way, step - 1)
-            if step < steps:
+            if step < steps - 1:
                 q_send(way, step)
+
+    far_sends = []
+
+    def far_out(origin, kind, peer):
+        ref = wq.at[origin, :, qpart]
+        copy = copy_to(ref, ref, far_s.at[kind], far_r.at[0], seq=peer)
+
+        @pl.when(inner)
+        def _():
+            copy.start()
+        far_sends.append((inner, copy))
+
+    def far_side():
+        far_out(at(toward), 0, beside)
+
+    def far_feed():
+        far_out(at(3 * toward), 1, spot(place - toward))
+
+    def far_copy():
+        ref = wq.at[at(steps), :, qpart]
+        return (copy_to(ref, ref, far_s.at[0], far_r.at[0], seq=beside),
+            copy_to(ref, ref, far_xs.at[0], far_xr.at[0], groups=other_group))
+
+    def far_cross(role):
+        landed, crossing = far_copy()
+
+        @pl.when(role)
+        def _():
+            landed.wait_recv()
+            crossing.start()
 
     orows = wo.shape[1] // 2
     ocut = (orows // 2 + 15) // 16 * 16
@@ -350,8 +374,6 @@
             def _():
                 copy.start()
             o_sends.append((cond, copy))
-
-    near = steps // 2
 
     def o_step(step):
         for way in (0, 1):
@@ -403,9 +425,10 @@
         ref = wo.at[lax.rem(origin, steps), feed_part]
         return holds(origin), copy_to(ref, ref, feed_s.at[index], feed_r.at[index], seq=spot(place - toward))
 
-    def feed_send():
-        for index, origin in enumerate((
-            at(2 * toward), spot(beside_place - toward), spot(beside_place - 2 * toward))):
+    def feed_send(which):
+        origins = (at(2 * toward), spot(beside_place - toward), spot(beside_place - 2 * toward))
+        for index in which:
+            origin = origins[index]
             cond, copy = feed_copy(origin, index)
 
             @pl.when(inner & cond)
@@ -457,6 +480,8 @@
             ag_send(way, 0, piece ^ way)
     o_begin()
     side_send(0)
+    for copy in wq_copies:
+        copy.wait()
     process(me)
     for i in range(0, width, 128):
         size = min(128, width - i)
@@ -470,6 +495,7 @@
         if step <= near:
             o_step(step)
         else:
+            q_begin()
             o_crossed(step - near - 1)
             side_send(1)
         process(at(-step))
@@ -480,7 +506,6 @@
 
     o_crossed(1)
     side_send(2)
-    q_begin()
     pos = {0: 1, 1: 2, 2: 3, 3: 4}
     half = dn.shape[1]
     chunk = CAP
@@ -497,15 +522,18 @@
                 up = proj[r, half:]
                 act[j % 2, r, :] = (gate * jax.nn.sigmoid(1.702 * gate) * (up + 1.0)).astype(jnp.bfloat16)
 
-            if j < steps:
-                q_step(j + 1)
+            if j in (1, 2):
+                q_step((1, 2).index(j) + 1)
+                if j == 1:
+                    far_side()
         dn_copies[2 * e].wait()
         dn_copies[2 * e + 1].wait()
         result = dot(act[0], dn[2 * e]) + dot(act[1], dn[2 * e + 1])
         done[:, e * CAP : (e + 1) * CAP, :] = result.astype(jnp.bfloat16).reshape(count, CAP, width)
-    for step in range(2 * own + 1, steps + 1):
-        q_step(step)
-
+
+    q_step(3)
+    far_cross(inner)
+    far_feed()
     hrows = tok_count // 2
     tail = width % 128
     full = width - tail
@@ -565,13 +593,15 @@
     part(me)
     for hop in range(3):
         side_wait(hop)
-    feed_send()
+    feed_send((0, 1, 2))
     rs_send(0, 1, 0)
     rs_send(1, 1, 1)
     for step in range(2, steps):
         for piece in (0, 1):
             for way in (0, 1):
                 rs_send(way, step, 1 ^ piece ^ way)
+        if step == 2:
+            far_cross(corner)
         feed_cross(step - 2)
     feed_cross(2)
     for c in (0, 1):
@@ -600,6 +630,7 @@
 
     for key in qx:
         qx[key].wait_recv()
+    far_copy()[1].wait_recv()
 
     def project(m, columns):
         total = None
@@ -708,7 +739,8 @@
     last.wait_send()
     for _, copy in sends:
         copy.wait_send()
-    for cond, copy in o_sends:
+    far_copy()[1].wait_send()
+    for cond, copy in o_sends + far_sends:
         @pl.when(cond)
         def _():
             copy.wait_send()
@@ -763,6 +795,7 @@
             dma((2, steps, 2)), dma((2, steps, 2)), dma((2, steps, 2)), dma((3, steps, 2)),
             dma((2, steps)), dma((2, steps)), dma((2, steps)), dma((2, steps)),
             dma((2, steps)), dma((2, steps)), dma((2, steps)), dma((2, steps)),
+            dma((2,)), dma((1,)), dma((1,)), dma((1,)),
             dma((3,)), dma((3,)), dma((3,)), dma((3,)), dma((3,)), dma((3,)), dma((2,)), dma((2,)), dma((2,)), dma((2,)),
         ],
         compiler_params=pltpu.CompilerParams(

time: 117 us -> 111 us (0.949); the launches traced: 116 us -> 111 us
  Pallas kernels: 114 us -> 109 us
    pallas_call x1, Pallas kernels: 114 us -> 109 us  [whole_layer(): pl.pallas_call(layer_kernel, out_shape=jax.ShapeDtypeStruct((width, tok_c...]
where the time goes in v6:
time: 111 us
  Pallas kernels  109 us (98%)
  local copies, waits for them, and re-layouts  1.75 us (2%)
    pallas_call x1, Pallas kernels, whole_layer(): pl.pallas_call(layer_kernel, out_shape=jax.ShapeDtypeStruct((width, tok_c...  109 us

profile of v6, /device:TPU:0, one launch (start us, length us, event | category | flops | bytes accessed | tf_op | source)
XLA Modules:
  0.0 111.1 jit_solution(4290237323577288723)
XLA Ops:
  0.0 109.3 %shard_map.100 = bf16[1440,128]{1,0:T(8,128)(2,1)} custom-call(bf16[1440,128]{1,0:T(8,128)(2,1)} %bitcast.15, s32[4,128]{1,0:T(4,128)} %bitcast.16, f32[4,128]{1,0:T(4,128)} %bitcast.17, f32[1440]{0:T(1024)} %gain_ref.1, f32[1440]{0:T(1024)} %attn_gain_ref.1, f32[32]{0:T(128)} %sink_ref.1, bf16[4,1440,1440]{2,1,0:T(8,128)(2,1)} %gate_up_ref.1, ...), custom_call_target="tpu_custom_call" | custom-call | tf_op jit(solution)/shard_map/pallas_call | solution.py:766
  109.3 1.7 %copy.12 = bf16[1,128,1440]{1,2,0:T(8,128)(2,1)} copy(bf16[1,128,1440]{1,2,0:T(8,128)(2,1)} %bitcast.13) | data formatting | bytes 737280

commit v7 on v6

--- a/solution.py
+++ b/solution.py
@@ -257,22 +257,6 @@
         copy.start()
     gu_copies = [pltpu.make_async_copy(gate_up_ref.at[j], gu.at[j], gu_sem.at[j]) for j in range(2 * own)]
     dn_copies = [pltpu.make_async_copy(down_ref.at[j], dn.at[j], dn_sem.at[j]) for j in range(2 * own)]
-    for copy in gu_copies + dn_copies:
-        copy.start()
-
-    tall = tok_t_ref[...].astype(jnp.float32)
-    scale = lax.rsqrt(jnp.sum(tall * tall, axis=0, keepdims=True) / width + eps)
-    for i in range(0, width, 128):
-        size = min(128, width - i)
-        gain = jnp.broadcast_to(gain_ref[pl.ds(i, size)].reshape(1, size), (tok_count, size)).T
-        blocks[me, i : i + size, :] = (
-            tok_t_ref[i : i + size, :].astype(jnp.float32) * scale * gain
-        ).astype(jnp.bfloat16)
-    expert_row = lax.broadcasted_iota(jnp.int32, (E, tok_count), 0)
-    dense = jnp.zeros((E, tok_count), jnp.float32)
-    for j in range(TOP):
-        dense = dense + jnp.where(expert_row == routes_ref[j : j + 1, :], weights_ref[j : j + 1, :], 0.0)
-    blocks[me, width : width + E, :] = dense.astype(jnp.bfloat16)
 
     pl.semaphore_wait(barrier, 7)
 
@@ -475,10 +459,25 @@
         for e in range(own):
             picked[e, n] = rows[e * CAP : (e + 1) * CAP]
 
+    o_begin()
+    tall = tok_t_ref[...].astype(jnp.float32)
+    scale = lax.rsqrt(jnp.sum(tall * tall, axis=0, keepdims=True) / width + eps)
+    for i in range(0, width, 128):
+        size = min(128, width - i)
+        gain = jnp.broadcast_to(gain_ref[pl.ds(i, size)].reshape(1, size), (tok_count, size)).T
+        blocks[me, i : i + size, :] = (
+            tok_t_ref[i : i + size, :].astype(jnp.float32) * scale * gain
+        ).astype(jnp.bfloat16)
+    expert_row = lax.broadcasted_iota(jnp.int32, (E, tok_count), 0)
+    dense = jnp.zeros((E, tok_count), jnp.float32)
+    for j in range(TOP):
+        dense = dense + jnp.where(expert_row == routes_ref[j : j + 1, :], weights_ref[j : j + 1, :], 0.0)
+    blocks[me, width : width + E, :] = dense.astype(jnp.bfloat16)
     for piece in (0, 1):
         for way in (0, 1):
             ag_send(way, 0, piece ^ way)
-    o_begin()
+    for copy in gu_copies[:2]:
+        copy.start()
     side_send(0)
     for copy in wq_copies:
         copy.wait()
@@ -498,6 +497,8 @@
             q_begin()
             o_crossed(step - near - 1)
             side_send(1)
+        for copy in (gu_copies[2:], dn_copies[:2], dn_copies[2:])[step - 1]:
+            copy.start()
         process(at(-step))
         process(at(step))
     ag[0, steps - 1, 0].wait_recv()
@@ -522,18 +523,15 @@
                 up = proj[r, half:]
                 act[j % 2, r, :] = (gate * jax.nn.sigmoid(1.702 * gate) * (up + 1.0)).astype(jnp.bfloat16)
 
-            if j in (1, 2):
-                q_step((1, 2).index(j) + 1)
-                if j == 1:
+            if j in (0, 2):
+                q_step((0, 2).index(j) + 1)
+                if j == 0:
                     far_side()
         dn_copies[2 * e].wait()
         dn_copies[2 * e + 1].wait()
         result = dot(act[0], dn[2 * e]) + dot(act[1], dn[2 * e + 1])
         done[:, e * CAP : (e + 1) * CAP, :] = result.astype(jnp.bfloat16).reshape(count, CAP, width)
 
-    q_step(3)
-    far_cross(inner)
-    far_feed()
     hrows = tok_count // 2
     tail = width % 128
     full = width - tail
@@ -584,6 +582,9 @@
     part(at(steps))
     rs_send(0, 0, 0)
     rs_send(1, 0, 1)
+    q_step(3)
+    far_cross(inner)
+    far_feed()
     for way in (0, 1):
         part(at((steps - 1) * (1 if way == 0 else -1)))
         rs_send(way, 1, 1 - way)
@@ -651,8 +652,9 @@
     packed = project(None, pl.ds(2 * kw, qw)).astype(jnp.bfloat16)
     queries[...] = (packed * (float(HEAD_SIZE) ** -0.5)).reshape(2, tok_count, qw)
 
-    lane = lax.broadcasted_iota(jnp.int32, (tok_count, 2 * tok_count), 1)
-    row = lax.broadcasted_iota(jnp.int32, (tok_count, 2 * tok_count), 0)
+    wide = (4 * tok_count, 2 * tok_count)
+    lane = lax.broadcasted_iota(jnp.int32, wide, 1)
+    row = lax.rem(lax.broadcasted_iota(jnp.int32, wide, 0), tok_count)
     left = lane < tok_count
     past = jnp.where(left, lane, lane - tok_count) > row
     low = lax.broadcasted_iota(jnp.int32, (tok_count, 2 * HEAD_SIZE), 1) < HEAD_SIZE
@@ -675,20 +677,23 @@
             v_own = stacked(kv[m, :, kw:], head)
             k_past = stacked(past_kv[:, :kw], head)
             v_past = stacked(past_kv[:, kw:], head)
-            for t in range(head * per_head, (head + 1) * per_head):
-                first_head = core * 2 * tiles + 2 * t
-                sink_a = jnp.exp(jnp.full((1, 1), sink_ref[first_head]))
-                sink_b = jnp.exp(jnp.full((1, 1), sink_ref[first_head + 1]))
-                x = queries[m, :, t * 128 : (t + 1) * 128]
+            for first in range(head * per_head, (head + 1) * per_head, 4):
+                some = range(first, first + 4)
+                sinks = [jnp.exp(jnp.concatenate(
+                    [jnp.full((tok_count, 1), sink_ref[core * 2 * tiles + 2 * t + side]) for t in some], axis=0))
+                    for side in (0, 1)]
+                x = jnp.concatenate([queries[m, :, t * 128 : (t + 1) * 128] for t in some], axis=0)
                 score = jnp.where(past, dot(x, k_past, ((1,), (1,))), dot(x, k_own, ((1,), (1,))))
                 weight = jnp.where(dropped, 0.0, jnp.exp(score))
-                mass_a = jnp.sum(weight[:, :tok_count], axis=1, keepdims=True) + sink_a
-                mass_b = jnp.sum(weight[:, tok_count:], axis=1, keepdims=True) + sink_b
+                mass_a = jnp.sum(weight[:, :tok_count], axis=1, keepdims=True) + sinks[0]
+                mass_b = jnp.sum(weight[:, tok_count:], axis=1, keepdims=True) + sinks[1]
                 probs = weight * jnp.where(left, 1.0 / mass_a, 1.0 / mass_b)
-                mixed[m, :, t * 128 : (t + 1) * 128] = (
+                result = (
                     dot(jnp.where(past, 0.0, probs).astype(jnp.bfloat16), v_own)
                     + dot(jnp.where(past, probs, 0.0).astype(jnp.bfloat16), v_past)
                 ).astype(jnp.bfloat16)
+                for k, t in enumerate(some):
+                    mixed[m, :, t * 128 : (t + 1) * 128] = result[k * tok_count : (k + 1) * tok_count]
 
     share = wo.shape[2]
     last = copy_to(given, back, pair_s.at[1], pair_r.at[1], pipe=other_core)

time: 111 us -> 107 us (0.964)
  Pallas kernels: 109 us -> 105 us
    pallas_call x1, Pallas kernels: 109 us -> 105 us  [whole_layer(): pl.pallas_call(layer_kernel, out_shape=jax.ShapeDtypeStruct((width, tok_c...]
where the time goes in v7:
time: 107 us
  Pallas kernels  105 us (98%)
  local copies, waits for them, and re-layouts  1.75 us (2%)
    pallas_call x1, Pallas kernels, whole_layer(): pl.pallas_call(layer_kernel, out_shape=jax.ShapeDtypeStruct((width, tok_c...  105 us

profile of v7, /device:TPU:0, one launch (start us, length us, event | category | flops | bytes accessed | tf_op | source)
XLA Modules:
  0.0 107.1 jit_solution(10796553458164123290)
XLA Ops:
  0.0 105.4 %shard_map.100 = bf16[1440,128]{1,0:T(8,128)(2,1)} custom-call(bf16[1440,128]{1,0:T(8,128)(2,1)} %bitcast.15, s32[4,128]{1,0:T(4,128)} %bitcast.16, f32[4,128]{1,0:T(4,128)} %bitcast.17, f32[1440]{0:T(1024)} %gain_ref.1, f32[1440]{0:T(1024)} %attn_gain_ref.1, f32[32]{0:T(128)} %sink_ref.1, bf16[4,1440,1440]{2,1,0:T(8,128)(2,1)} %gate_up_ref.1, ...), custom_call_target="tpu_custom_call" | custom-call | tf_op jit(solution)/shard_map/pallas_call | solution.py:771
  105.4 1.7 %copy.12 = bf16[1,128,1440]{1,2,0:T(8,128)(2,1)} copy(bf16[1,128,1440]{1,2,0:T(8,128)(2,1)} %bitcast.13) | data formatting | bytes 737280

commit v8 on v7

--- a/solution.py
+++ b/solution.py
@@ -687,7 +687,7 @@
                 weight = jnp.where(dropped, 0.0, jnp.exp(score))
                 mass_a = jnp.sum(weight[:, :tok_count], axis=1, keepdims=True) + sinks[0]
                 mass_b = jnp.sum(weight[:, tok_count:], axis=1, keepdims=True) + sinks[1]
-                probs = weight * jnp.where(left, 1.0 / mass_a, 1.0 / mass_b)
+                probs = (weight * 0.125) * jnp.where(left, 1.0 / (mass_a * 0.125), 1.0 / (mass_b * 0.125))
                 result = (
                     dot(jnp.where(past, 0.0, probs).astype(jnp.bfloat16), v_own)
                     + dot(jnp.where(past, probs, 0.0).astype(jnp.bfloat16), v_past)

time: 107 us -> 107 us (level)
  no operation moved by 1% of the time
where the time goes in v8:
time: 107 us
  Pallas kernels  105 us (98%)
  local copies, waits for them, and re-layouts  1.75 us (2%)
    pallas_call x1, Pallas kernels, whole_layer(): pl.pallas_call(layer_kernel, out_shape=jax.ShapeDtypeStruct((width, tok_c...  105 us

profile of v8, /device:TPU:0, one launch (start us, length us, event | category | flops | bytes accessed | tf_op | source)
XLA Modules:
  0.0 107.2 jit_solution(17055552265226772173)
XLA Ops:
  0.0 105.4 %shard_map.100 = bf16[1440,128]{1,0:T(8,128)(2,1)} custom-call(bf16[1440,128]{1,0:T(8,128)(2,1)} %bitcast.15, s32[4,128]{1,0:T(4,128)} %bitcast.16, f32[4,128]{1,0:T(4,128)} %bitcast.17, f32[1440]{0:T(1024)} %gain_ref.1, f32[1440]{0:T(1024)} %attn_gain_ref.1, f32[32]{0:T(128)} %sink_ref.1, bf16[4,1440,1440]{2,1,0:T(8,128)(2,1)} %gate_up_ref.1, ...), custom_call_target="tpu_custom_call" | custom-call | tf_op jit(solution)/shard_map/pallas_call | solution.py:771
  105.4 1.7 %copy.12 = bf16[1,128,1440]{1,2,0:T(8,128)(2,1)} copy(bf16[1,128,1440]{1,2,0:T(8,128)(2,1)} %bitcast.13) | data formatting | bytes 737280

commit v9 on v8

--- a/solution.py
+++ b/solution.py
@@ -585,6 +585,9 @@
     q_step(3)
     far_cross(inner)
     far_feed()
+    for hop in range(3):
+        side_wait(hop)
+    feed_send((0, 1, 2))
     for way in (0, 1):
         part(at((steps - 1) * (1 if way == 0 else -1)))
         rs_send(way, 1, 1 - way)
@@ -592,9 +595,6 @@
         part(at(offset))
         part(at(-offset))
     part(me)
-    for hop in range(3):
-        side_wait(hop)
-    feed_send((0, 1, 2))
     rs_send(0, 1, 0)
     rs_send(1, 1, 1)
     for step in range(2, steps):

time: 107 us -> 107 us (level)
  no operation moved by 1% of the time
where the time goes in v9:
time: 107 us
  Pallas kernels  105 us (98%)
  local copies, waits for them, and re-layouts  1.75 us (2%)
    pallas_call x1, Pallas kernels, whole_layer(): pl.pallas_call(layer_kernel, out_shape=jax.ShapeDtypeStruct((width, tok_c...  105 us

profile of v9, /device:TPU:0, one launch (start us, length us, event | category | flops | bytes accessed | tf_op | source)
XLA Modules:
  0.0 107.2 jit_solution(12696327806984241112)
XLA Ops:
  0.0 105.4 %shard_map.100 = bf16[1440,128]{1,0:T(8,128)(2,1)} custom-call(bf16[1440,128]{1,0:T(8,128)(2,1)} %bitcast.15, s32[4,128]{1,0:T(4,128)} %bitcast.16, f32[4,128]{1,0:T(4,128)} %bitcast.17, f32[1440]{0:T(1024)} %gain_ref.1, f32[1440]{0:T(1024)} %attn_gain_ref.1, f32[32]{0:T(128)} %sink_ref.1, bf16[4,1440,1440]{2,1,0:T(8,128)(2,1)} %gate_up_ref.1, ...), custom_call_target="tpu_custom_call" | custom-call | tf_op jit(solution)/shard_map/pallas_call | solution.py:771
  105.4 1.7 %copy.12 = bf16[1,128,1440]{1,2,0:T(8,128)(2,1)} copy(bf16[1,128,1440]{1,2,0:T(8,128)(2,1)} %bitcast.13) | data formatting | bytes 737280
